TPU v7x, 32 devices: a whole 2x2x4 slice. The times are simulated.
32 devices in a mesh: grid: 4 (over x, core), comp: 8 (over z, y).
Axes of the slice: x: 2, y: 2, z: 4, core: 2. Of those that a mesh axis runs over, the one named last changes fastest.
Arguments:
- spectra: float32 [32, 32, 36, 2048], P('comp', None, None, 'grid'), may hold values from 0.1 to 2
- u_wind: float32 [32, 2048], P(None, 'grid'), may hold values from 2 to 20
- wind_dir: float32 [32, 2048], P(None, 'grid'), may hold values from -3.140625 to 3.140625
- sea_mask: int32 [32, 2048], P(None, 'grid'), may hold values from 0 to 1, as said below
Outputs:
- spectra_next: float32 [32, 32, 36, 2048], P('comp', None, None, 'grid')
Inputs may be any that keep to these rules, and one draw needn't show every extreme that they name: sea_mask is 1 at sea and 0 on land; land lies in rectangular blocks of rows and columns.
All inputs are finite; a program needn't handle non-finite values.
Results may differ from a plain program's by a relative error of at most 0.00016.
Values sent between devices are 32-bit elements; how exact they have to be, the bound alone decides.
No kernel may reach another device: no remote copies, remote signals or barrier semaphores. Data moves between devices by JAX's collectives and lax.ppermute only.
A program may use at most 192 MiB of HBM per device.

v0:
```python
import functools
import math

import jax
import jax.numpy as jnp
import numpy as np
from jax import lax
from jax.experimental import pallas as pl
from jax.experimental.pallas import tpu as pltpu
from jax.sharding import PartitionSpec as P


GRAVITY = 9.81
FREQ_LOW = 0.04
FREQ_RATIO = 1.1
LAMBDA = 0.25
SOURCE_STEP = 120.0
ADVECT_STEP = 220.0
WIND_FACTOR = 0.0003125
TRANSFER_FACTOR = 0.1
EARTH_RADIUS = 6371000.0
BAND_CENTRE = 30.0
CELL_DEGREES = 0.05
CELL_RADIANS = CELL_DEGREES * math.pi / 180.0
ANGLE_NEAR = 11.48
ANGLE_FAR = 33.56
FREQ_UPPER_SHIFT = math.log(1.0 + LAMBDA) / math.log(FREQ_RATIO)
FREQ_LOWER_SHIFT = math.log(1.0 - LAMBDA) / math.log(FREQ_RATIO)
WEIGHT_UPPER = 1.0 / (1.0 + LAMBDA) ** 4
WEIGHT_LOWER = 1.0 / (1.0 - LAMBDA) ** 4
WEIGHT_CROSS = 2.0 / (1.0 - LAMBDA * LAMBDA) ** 4

LANES = 128
VMEM_LIMIT = 60 * 1024 * 1024


def taps(shift):
    low = math.floor(shift)
    part = shift - low
    return ((low, 1.0 - part), (low + 1, part))


UP_TAPS = taps(FREQ_UPPER_SHIFT)
DOWN_TAPS = taps(FREQ_LOWER_SHIFT)
REACH_HIGH = UP_TAPS[1][0]
REACH_LOW = -DOWN_TAPS[0][0]
REACH = REACH_HIGH + REACH_LOW


def pick(values, index):
    chosen = values[0]
    for place in range(1, len(values)):
        chosen = jnp.where(index == place, values[place], chosen)
    return chosen


def sub_rows(rows):
    return 8 if rows % 8 == 0 else rows


SPOT, GROUP_FIRST, OWN_FIRST, EVEN, HAS_BELOW, HAS_ABOVE = range(6)
BELOW, HERE, ABOVE = range(3)


def pack_kernel(parts, rows, low, size, lean, scalars, x_ref, mask_ref, *outs):
    spot = scalars[SPOT]
    mask = mask_ref[...].astype(jnp.float32)
    starts = [b * rows + low for b in range(parts)]
    freqs = x_ref.shape[0]
    for f in range(freqs):
        blocks = [x_ref[f, :, s : s + size, :] * mask[None, s : s + size, :] for s in starts]
        for turn in range(parts):
            outs[turn][f] = pick(blocks, lax.rem(spot + turn, parts))
    if lean:
        even = scalars[EVEN]
        outs[parts][...] = outs[0][pl.ds(even, freqs - 1)]
        outs[parts + 1][...] = outs[0][pl.ds(1 - even, freqs - 1)]


def pack(scalars, spectra, sea_mask, chunk, parts, lean):
    column, low, size = chunk
    freqs, dirs, total_rows, _ = spectra.shape
    rows = total_rows // parts

    def shape(count):
        return jax.ShapeDtypeStruct((count, dirs, size, LANES), jnp.float32)

    counts = [freqs] * parts + [freqs - 1] * (2 if lean else 0)
    return pl.pallas_call(
        functools.partial(pack_kernel, parts, rows, low, size, lean),
        out_shape=[shape(count) for count in counts],
        grid=(1,),
        in_specs=[
            pl.BlockSpec(memory_space=pltpu.SMEM),
            pl.BlockSpec((freqs, dirs, total_rows, LANES), lambda i: (0, 0, 0, column)),
            pl.BlockSpec((total_rows, LANES), lambda i: (0, column)),
        ],
        out_specs=[
            pl.BlockSpec((count, dirs, size, LANES), lambda i: (0, 0, 0, 0)) for count in counts
        ],
        compiler_params=pltpu.CompilerParams(vmem_limit_bytes=VMEM_LIMIT),
    )(scalars, spectra, sea_mask)


def join_kernel(freqs, scalars, own_ref, other_ref, a_ref, b_ref, sems):
    even, spot = scalars[EVEN], scalars[SPOT]
    for side, (out_ref, up) in enumerate(((a_ref, even), (b_ref, 1 - even))):
        rest = pltpu.make_async_copy(
            other_ref.at[pl.ds(up, freqs - 1)], out_ref.at[pl.ds(up, freqs - 1)], sems.at[side, 0]
        )
        rest.start()
        place = (1 - up) * (freqs - 1)
        from_own = spot == up

        @pl.when(from_own)
        def _():
            pltpu.make_async_copy(own_ref.at[place], out_ref.at[place], sems.at[side, 1]).start()

        @pl.when(jnp.logical_not(from_own))
        def _():
            pltpu.make_async_copy(other_ref.at[place], out_ref.at[place], sems.at[side, 1]).start()

    for side, out_ref in enumerate((a_ref, b_ref)):
        pltpu.make_async_copy(
            other_ref.at[pl.ds(0, freqs - 1)], out_ref.at[pl.ds(0, freqs - 1)], sems.at[side, 0]
        ).wait()
        pltpu.make_async_copy(other_ref.at[0], out_ref.at[0], sems.at[side, 1]).wait()


def join(scalars, own, other):
    anywhere = pl.BlockSpec(memory_space=pl.ANY)
    shape = jax.ShapeDtypeStruct(own.shape, own.dtype)
    return pl.pallas_call(
        functools.partial(join_kernel, own.shape[0]),
        out_shape=[shape] * 2,
        grid=(1,),
        in_specs=[pl.BlockSpec(memory_space=pltpu.SMEM), anywhere, anywhere],
        out_specs=[pl.BlockSpec(own.shape, lambda i: (0, 0, 0, 0))] * 2,
        scratch_shapes=[pltpu.SemaphoreType.DMA((2, 2))],
    )(scalars, own, other)


def source_kernel(parts, freqs, dirs, rows, low, size, lean, cuts, scalars, gain_ref, drop_ref,
                  along_ref, across_ref, *refs):
    count = parts + (4 if lean else 2 * parts)
    ins, outs = refs[:count], refs[count : count + parts * cuts]
    (window, wind, back_up, back_down, centre, post, in_sems, out_sems) = refs[
        count + parts * cuts :
    ]
    spot = scalars[SPOT]
    even = scalars[EVEN]
    first = scalars[GROUP_FIRST]
    span = parts * freqs
    step = sub_rows(size)
    pieces = size // step

    def block_of(turn):
        return lax.rem(spot + parts - turn, parts)

    def fetches(piece):
        moves = [(ins[turn], 0, freqs, HERE * span + block_of(turn) * freqs) for turn in range(parts)]
        for side in range(2):
            above = even if side == 0 else 1 - even
            base = above * (ABOVE * span)
            if lean:
                near, rest = ins[parts + 2 * side], ins[parts + 2 * side + 1]
                skip = 1 - above
                moves += [
                    (near, 0, freqs - 1, base + spot * freqs + skip),
                    (rest, skip, freqs - 1, base + (1 - spot) * freqs + skip),
                    (rest, above * (freqs - 1), 1, base + freqs - above),
                ]
            else:
                moves += [
                    (ins[parts * (1 + side) + turn], 0, freqs, base + block_of(turn) * freqs)
                    for turn in range(parts)
                ]
        return [
            pltpu.make_async_copy(
                ref.at[pl.ds(start, length), :, pl.ds(piece * step, step), :],
                window.at[piece, pl.ds(place, length)],
                in_sems.at[piece, index],
            )
            for index, (ref, start, length, place) in enumerate(moves)
        ]

    share = freqs // cuts

    def stores(piece):
        return [
            pltpu.make_async_copy(
                post.at[piece, pl.ds(block_of(turn) * freqs + cut * share, share)],
                outs[turn * cuts + cut].at[:, :, pl.ds(piece * step, step), :],
                out_sems.at[piece, turn * cuts + cut],
            )
            for turn in range(parts)
            for cut in range(cuts)
        ]

    for piece in range(pieces):
        for copy in fetches(piece):
            copy.start()

    scale_up = TRANSFER_FACTOR * WEIGHT_UPPER
    scale_down = TRANSFER_FACTOR * WEIGHT_LOWER
    cross = TRANSFER_FACTOR * WEIGHT_CROSS / (scale_up * scale_down)
    near = taps(ANGLE_NEAR * dirs / 360.0)
    far = taps(ANGLE_FAR * dirs / 360.0)

    starts = [b * rows + low for b in range(parts)]
    along = pick([along_ref[s : s + size, :] for s in starts], spot)
    across = pick([across_ref[s : s + size, :] for s in starts], spot)

    for piece in range(pieces):
        at = piece * step
        for j in range(dirs):
            angle = 2.0 * math.pi * j / dirs
            wind[j] = along[at : at + step] * math.cos(angle) + across[at : at + step] * math.sin(angle)
        for copy in fetches(piece):
            copy.wait()

        for flag, group in ((HAS_BELOW, BELOW), (HAS_ABOVE, ABOVE)):

            @pl.when(scalars[flag] == 0)
            def _(group=group):
                def clear(f, carry):
                    window[piece, group * span + f] = jnp.zeros(window.shape[2:], jnp.float32)
                    return carry

                lax.fori_loop(0, span, clear, 0)

        def delta_step(index, carry):
            k = span - REACH_HIGH + index

            @functools.cache
            def energy(j):
                return window[piece, k, j]

            @functools.cache
            def upper(j):
                (o0, w0), (o1, w1) = UP_TAPS
                return (scale_up * w0) * window[piece, k + o0, j] + (scale_up * w1) * window[
                    piece, k + o1, j
                ]

            @functools.cache
            def lower(j):
                (o0, w0), (o1, w1) = DOWN_TAPS
                return (scale_down * w0) * window[piece, k + o0, j] + (scale_down * w1) * window[
                    piece, k + o1, j
                ]

            @functools.cache
            def delta(sign, j):
                plus = sum(w * upper((j + sign * o) % dirs) for o, w in near)
                minus = sum(w * lower((j - sign * o) % dirs) for o, w in far)
                value = energy(j)
                return value * (value * (plus + minus) - cross * (plus * minus))

            for j in range(dirs):
                back_up[index, j] = sum(
                    w * (delta(1, (j - o) % dirs) + delta(-1, (j + o) % dirs)) for o, w in near
                )
                back_down[index, j] = sum(
                    w * (delta(1, (j + o) % dirs) + delta(-1, (j - o) % dirs)) for o, w in far
                )
                centre[index, j] = -2.0 * (delta(1, j) + delta(-1, j))
            return carry

        lax.fori_loop(0, span + REACH, delta_step, 0)

        def out_step(m, carry):
            gain = gain_ref[first + m]
            drop = drop_ref[first + m]
            index = m + REACH_HIGH
            for j in range(dirs):
                value = window[piece, span + m, j]
                total = value * (1.0 + jnp.maximum(0.0, gain * wind[j] - drop)) + centre[index, j]
                for o, w in UP_TAPS:
                    total = total + w * back_up[index - o, j]
                for o, w in DOWN_TAPS:
                    total = total + w * back_down[index - o, j]
                post[piece, m, j] = total
            return carry

        lax.fori_loop(0, span, out_step, 0)
        for copy in stores(piece):
            copy.start()
    for piece in range(pieces):
        for copy in stores(piece):
            copy.wait()


def source(scalars, gain, drop, along, across, operands, chunk, parts, freqs, lean, cuts):
    column, low, size = chunk
    dirs = operands[0].shape[1]
    total_rows = along.shape[0]
    rows = total_rows // parts
    span = parts * freqs
    step = sub_rows(size)
    pieces = size // step
    shape = jax.ShapeDtypeStruct((freqs // cuts, dirs, size, LANES), jnp.float32)
    smem = pl.BlockSpec(memory_space=pltpu.SMEM)
    anywhere = pl.BlockSpec(memory_space=pl.ANY)
    wind_spec = pl.BlockSpec((total_rows, LANES), lambda i: (0, column))
    inner = (dirs, step, LANES)
    return pl.pallas_call(
        functools.partial(source_kernel, parts, freqs, dirs, rows, low, size, lean, cuts),
        out_shape=[shape] * (parts * cuts),
        grid=(1,),
        in_specs=[smem, smem, smem, wind_spec, wind_spec] + [anywhere] * len(operands),
        out_specs=[anywhere] * (parts * cuts),
        scratch_shapes=[
            pltpu.VMEM((pieces, 3 * span) + inner, jnp.float32),
            pltpu.VMEM(inner, jnp.float32),
            pltpu.VMEM((span + REACH,) + inner, jnp.float32),
            pltpu.VMEM((span + REACH,) + inner, jnp.float32),
            pltpu.VMEM((span + REACH,) + inner, jnp.float32),
            pltpu.VMEM((pieces, span) + inner, jnp.float32),
            pltpu.SemaphoreType.DMA((pieces, parts + 2 * max(3, parts))),
            pltpu.SemaphoreType.DMA((pieces, parts * cuts)),
        ],
        compiler_params=pltpu.CompilerParams(vmem_limit_bytes=VMEM_LIMIT),
    )(scalars, gain, drop, along, across, *operands)


def face_weights(courant, forward):
    curve = (courant * courant - 1.0) * (1.0 / 6.0)
    half = 0.5 * courant
    if forward:
        return (courant * curve, courant * (0.5 + half - 2.0 * curve), courant * (0.5 - half + curve))
    return (courant * (0.5 + half + curve), courant * (0.5 - half - 2.0 * curve), courant * curve)


EDGE = 8


def sweep_kernel(parts, layout, dirs, rows, start, aliased, scalars, speed_ref, cos_ref, sin_ref,
                 geo_ref, mask_ref, *refs):
    tiles = len(layout) - 2
    count = sum(len(pieces) for pieces in layout) * parts
    ins = refs[:count]
    out_ref, buffer = refs[count + aliased :]
    spot = scalars[SPOT]
    total_rows = rows * parts
    speed = speed_ref[scalars[OWN_FIRST] + start + pl.program_id(0)]
    lane = lax.broadcasted_iota(jnp.int32, (total_rows, LANES), 1)
    row_zero = jnp.zeros((EDGE, LANES), jnp.float32)
    slots = buffer.shape[0]
    for slot in range(slots):
        for tile in range(tiles):
            buffer[slot, tile, :EDGE] = row_zero
            buffer[slot, tile, EDGE + total_rows :] = row_zero

    def column(tile, j):
        at = sum(len(pieces) for pieces in layout[:tile]) * parts
        pieces = []
        for index in range(len(layout[tile])):
            blocks = [ins[at + index * parts + turn][0, j] for turn in range(parts)]
            pieces.append([pick(blocks, lax.rem(b + parts - spot, parts)) for b in range(parts)])
        return jnp.concatenate([piece[b] for b in range(parts) for piece in pieces], axis=0)

    def one(j, forward, northward, slot):
        cells = [column(tile, j) for tile in range(tiles + 2)]
        weights = face_weights((speed * cos_ref[j]) * geo_ref[0], forward)
        moved = [pltpu.roll(cell, 1, axis=1) for cell in cells]
        steps = [cells[0] - moved[0]]
        for tile in range(1, tiles + 2):
            steps.append(cells[tile] - jnp.where(lane < 1, moved[tile - 1], moved[tile]))

        def ahead(amount):
            turned = [None] + [pltpu.roll(step, LANES - amount, axis=1) for step in steps[1:]]
            return [None] + [
                jnp.where(lane >= LANES - amount, turned[tile + 1], turned[tile])
                for tile in range(1, tiles + 1)
            ]

        if forward:
            turned = [pltpu.roll(step, 1, axis=1) for step in steps[:-1]]
            rear = [None] + [
                jnp.where(lane < 1, turned[tile - 1], turned[tile]) for tile in range(1, tiles + 1)
            ]
            spread = (rear, steps, ahead(1))
        else:
            spread = (steps, ahead(1), ahead(2))
        low, mid, high = face_weights(speed * sin_ref[j], northward)
        for tile in range(tiles):
            here = slice(tile * LANES, (tile + 1) * LANES)
            mask = mask_ref[:, here].astype(jnp.float32)
            swept = cells[tile + 1]
            for weight, value in zip(weights, spread):
                swept = swept - weight * value[tile + 1]
            swept = swept * mask
            buffer[slot, tile, EDGE : EDGE + total_rows] = swept

            def shifted(amount, tile=tile):
                return buffer[slot, tile, EDGE + amount : EDGE + amount + total_rows]

            under, over = shifted(-1), shifted(1)
            if northward:
                front = low * under + mid * swept + high * over
                rear_flux = low * shifted(-2) + mid * under + high * swept
            else:
                front = low * swept + mid * over + high * shifted(2)
                rear_flux = low * under + mid * swept + high * over
            out_ref[0, j, :, here] = (swept - geo_ref[1] * front + geo_ref[2] * rear_flux) * mask

    angles = [2.0 * math.pi * j / dirs for j in range(dirs)]
    kinds = [(round(math.cos(angle), 12) >= 0.0, round(math.sin(angle), 12) >= 0.0) for angle in angles]
    begin = 0
    while begin < dirs:
        end = begin
        while end < dirs and kinds[end] == kinds[begin]:
            end += 1
        kind = kinds[begin]
        whole = (end - begin) // slots

        def body(index, carry, kind=kind, begin=begin):
            for slot in range(slots):
                one(begin + index * slots + slot, *kind, slot)
            return carry

        lax.fori_loop(0, whole, body, 0)
        for j in range(begin + whole * slots, end):
            one(j, *kind, 0)
        begin = end


def sweep(scalars, speed, cosines, sines, geometry, sea_mask, layout, start, length, freqs, result):
    parts = len(layout[0][0])
    total_rows, width = sea_mask.shape
    dirs = cosines.shape[0]
    rows = total_rows // parts
    flat = [entry for pieces in layout for piece in pieces for entry in piece]
    smem = pl.BlockSpec(memory_space=pltpu.SMEM)

    def block(array, origin):
        offset = start - origin
        return pl.BlockSpec((1,) + array.shape[1:], lambda f: (f + offset, 0, 0, 0))

    operands = [array for array, _ in flat]
    specs = [block(array, origin) for array, origin in flat]
    aliases = {}
    if result is not None:
        aliases = {6 + len(operands): 0}
        operands.append(result)
        specs.append(pl.BlockSpec(memory_space=pl.ANY))
    return pl.pallas_call(
        functools.partial(
            sweep_kernel, parts, [[None] * len(pieces) for pieces in layout], dirs, rows, start,
            len(aliases),
        ),
        out_shape=jax.ShapeDtypeStruct((freqs, dirs, total_rows, width), jnp.float32),
        grid=(length,),
        in_specs=[smem] * 4
        + [
            pl.BlockSpec((3, total_rows, LANES), lambda f: (0, 0, 0)),
            pl.BlockSpec((total_rows, width), lambda f: (0, 0)),
        ]
        + specs,
        out_specs=pl.BlockSpec((1, dirs, total_rows, width), lambda f: (f + start, 0, 0, 0)),
        scratch_shapes=[
            pltpu.VMEM((2, width // LANES, total_rows + 2 * EDGE, LANES), jnp.float32)
        ],
        input_output_aliases=aliases,
        compiler_params=pltpu.CompilerParams(vmem_limit_bytes=VMEM_LIMIT),
    )(scalars, speed, cosines, sines, geometry, sea_mask, *operands)


def group_size(comp_count, freq_local, band_rows):
    for parts in range(1, comp_count + 1):
        if comp_count % parts == 0 and band_rows % parts == 0 and parts * freq_local >= REACH:
            return parts
    return comp_count


def chunk_list(tiles, rows):
    columns = [tiles - 1] + list(range(tiles - 1))
    chunks = [(column, 0, rows) for column in columns]
    if rows % 16 == 0:
        column = columns[-1]
        chunks[-1:] = [(column, 0, rows // 2), (column, rows // 2, rows // 2)]
    return chunks


def shards(spectra, u_wind, wind_dir, sea_mask):
    freq_local, band_rows, dir_count, lon_cells = spectra.shape
    comp_count = lax.axis_size("comp")
    grid_count = lax.axis_size("grid")
    parts = group_size(comp_count, freq_local, band_rows)
    lean = parts == 2
    groups = comp_count // parts
    comp_index = lax.axis_index("comp")
    spot = lax.rem(comp_index, parts)
    group = lax.div(comp_index, parts)
    scalars = jnp.stack(
        [
            spot,
            group * (parts * freq_local),
            comp_index * freq_local,
            1 - lax.rem(group, 2),
            (group > 0).astype(jnp.int32),
            (group < groups - 1).astype(jnp.int32),
        ]
    ).astype(jnp.int32)

    turns = []
    for turn in range(parts):
        turns.append([(i, i - i % parts + (i % parts + turn) % parts) for i in range(comp_count)])
    returns = [[(target, origin) for origin, target in pairs] for pairs in turns]

    def partners(other):
        pairs = []
        for g in range(grid_count):
            for i in range(comp_count):
                mate = other(i // parts)
                if 0 <= mate < groups:
                    target = g * comp_count + mate * parts + i % parts
                else:
                    target = (g ^ 1 if g ^ 1 < grid_count else g) * comp_count + i
                pairs.append((g * comp_count + i, target))
        return pairs

    sides = [partners(lambda g: g + 1 - 2 * (g % 2)), partners(lambda g: g - 1 + 2 * (g % 2))]
    eastward = [(i, i + 1) for i in range(grid_count - 1)]
    westward = [(i + 1, i) for i in range(grid_count - 1)]

    omega = 2.0 * math.pi * FREQ_LOW * FREQ_RATIO ** np.arange(freq_local * comp_count)
    factor = WIND_FACTOR * SOURCE_STEP
    gain = jnp.asarray(factor * omega * omega / GRAVITY, jnp.float32)
    drop = jnp.asarray(factor * omega, jnp.float32)
    speed = jnp.asarray(
        GRAVITY / (2.0 * omega) * ADVECT_STEP / (EARTH_RADIUS * CELL_RADIANS), jnp.float32
    )
    angles = 2.0 * math.pi * np.arange(dir_count) / dir_count
    cosines = jnp.asarray(np.cos(angles), jnp.float32)
    sines = jnp.asarray(np.sin(angles), jnp.float32)
    cells = np.cos(
        np.radians(BAND_CENTRE + (np.arange(band_rows) - (band_rows - 1) / 2.0) * CELL_DEGREES)
    )
    faces = np.cos(
        np.radians(BAND_CENTRE + (np.arange(band_rows + 1) - band_rows / 2.0) * CELL_DEGREES)
    )
    geometry = np.stack([1.0 / cells, faces[1:] / cells, faces[:-1] / cells])
    geometry = jnp.asarray(np.repeat(geometry[:, :, None], LANES, axis=2), jnp.float32)

    along = u_wind * jnp.cos(wind_dir)
    across = u_wind * jnp.sin(wind_dir)

    field = jnp.transpose(spectra, (0, 2, 1, 3))
    tiles = lon_cells // LANES
    rows = band_rows // parts
    chunks = chunk_list(tiles, rows)
    halves = 2 if freq_local % 2 == 0 else 1
    half = freq_local // halves

    both = ("grid", "comp")

    done = [[] for _ in range(tiles)]
    for index, chunk in enumerate(chunks):
        packed = pack(scalars, field, sea_mask, chunk, parts, lean)
        held = [packed[0]] + [
            lax.ppermute(packed[turn], "comp", turns[turn]) for turn in range(1, parts)
        ]
        operands = list(held)
        if lean:
            joined = join(scalars, held[0], held[1])
            for side, pairs in enumerate(sides):
                operands.append(lax.ppermute(packed[parts + side], both, pairs))
                operands.append(lax.ppermute(joined[side], both, pairs))
        else:
            for pairs in sides:
                for turn in range(parts):
                    operands.append(lax.ppermute(held[turn], both, pairs))
        cuts = halves if index == len(chunks) - 1 else 1
        post = source(
            scalars, gain, drop, along, across, operands, chunk, parts, freq_local, lean, cuts
        )
        piece = []
        for turn in range(parts):
            own = list(post[turn * cuts : (turn + 1) * cuts])
            if turn > 0:
                own = [lax.ppermute(value, "comp", returns[turn]) for value in own]
            piece.append(own)
        done[chunk[0]].append(piece)

    def border(column, pairs):
        return [
            [[lax.ppermute(value, "grid", pairs) for value in cuts] for cuts in piece]
            for piece in done[column]
        ]

    layout = [border(tiles - 1, eastward)] + done + [border(0, westward)]
    result = None
    for part in range(halves):
        entries = [
            [
                [
                    (cuts[part], part * half) if len(cuts) > 1 else (cuts[0], 0)
                    for cuts in piece
                ]
                for piece in pieces
            ]
            for pieces in layout
        ]
        result = sweep(
            scalars, speed, cosines, sines, geometry, sea_mask, entries, part * half, half,
            freq_local, result,
        )
    return jnp.transpose(result, (0, 2, 1, 3))


def solution(mesh):
    return jax.shard_map(
        shards,
        mesh=mesh,
        in_specs=(P("comp", None, None, "grid"), P(None, "grid"), P(None, "grid"), P(None, "grid")),
        out_specs=P("comp", None, None, "grid"),
        check_vma=False,
    )
```

profile of v0, /device:TPU:1, one launch (start us, length us, event | category | flops | bytes accessed | tf_op | source)
XLA Modules:
  0.0 308.0 jit_solution(3451404955565277102)
XLA Ops:
  0.0 0.6 stack.35.scalars
  0.6 3.1 %shard_map.112 = (f32[4,36,8,128]{3,2,1,0:T(8,128)}, f32[4,36,8,128]{3,2,1,0:T(8,128)}, f32[3,36,8,128]{3,2,1,0:T(8,128)}, f32[3,36,8,128]{3,2,1,0:T(8,128)}) custom-call(s32[6]{0:T(128)} %stack.35.scalars, f32[4,36,32,512]{3,2,1,0:T(8,128)} %bitcast.8, s32[32,512]{1,0:T(8,128)} %mask_ref.13), custom_call_target="tpu_custom_call" | custom-call | tf_op jit(solution)/shard_map/pallas_call | solution.py:89
  3.7 2.1 collective-permute-start.27
  5.8 1.0 collective-permute-start.29
  6.8 3.1 %shard_map.109 = (f32[4,36,8,128]{3,2,1,0:T(8,128)}, f32[4,36,8,128]{3,2,1,0:T(8,128)}, f32[3,36,8,128]{3,2,1,0:T(8,128)}, f32[3,36,8,128]{3,2,1,0:T(8,128)}) custom-call(s32[6]{0:T(128)} %stack.35.scalars, f32[4,36,32,512]{3,2,1,0:T(8,128)} %bitcast.9, s32[32,512]{1,0:T(8,128)} %mask_ref.13), custom_call_target="tpu_custom_call" | custom-call | tf_op jit(solution)/shard_map/pallas_call | solution.py:89
  9.9 1.6 collective-permute-start.21
  11.6 1.5 collective-permute-start.23
  13.1 1.2 collective-permute-start.26
  14.3 4.0 %shard_map.106 = (f32[4,36,16,128]{3,2,1,0:T(8,128)}, f32[4,36,16,128]{3,2,1,0:T(8,128)}, f32[3,36,16,128]{3,2,1,0:T(8,128)}, f32[3,36,16,128]{3,2,1,0:T(8,128)}) custom-call(s32[6]{0:T(128)} %stack.35.scalars, f32[4,36,32,512]{3,2,1,0:T(8,128)} %bitcast.10, s32[32,512]{1,0:T(8,128)} %mask_ref.13), custom_call_target="tpu_custom_call" | custom-call | tf_op jit(solution)/shard_map/pallas_call | solution.py:89
  18.4 1.6 collective-permute-start.17
  20.1 5.3 %collective-permute-done.21.refs_2_ = f32[3,36,8,128]{3,2,1,0:T(8,128)S(1)} collective-permute-done((f32[3,36,8,128]{3,2,1,0:T(8,128)}, f32[3,36,8,128]{3,2,1,0:T(8,128)S(1)}, u32[]{:S(2)}, u32[]{:S(2)}) %collective-permute-start.21) | collective-permute-done | bytes 442400 | tf_op jit(solution)/shard_map/ppermute | solution.py:569
  25.4 0.8 copy-done.20
  26.2 1.1 collective-permute-start.20
  27.3 3.9 %shard_map.103 = (f32[4,36,16,128]{3,2,1,0:T(8,128)}, f32[4,36,16,128]{3,2,1,0:T(8,128)}, f32[3,36,16,128]{3,2,1,0:T(8,128)}, f32[3,36,16,128]{3,2,1,0:T(8,128)}) custom-call(s32[6]{0:T(128)} %stack.35.scalars, f32[4,36,32,512]{3,2,1,0:T(8,128)} %bitcast.11, s32[32,512]{1,0:T(8,128)} %mask_ref.13), custom_call_target="tpu_custom_call" | custom-call | tf_op jit(solution)/shard_map/pallas_call | solution.py:89
  31.3 1.4 collective-permute-start.9
  32.9 4.0 %shard_map.100 = (f32[4,36,16,128]{3,2,1,0:T(8,128)}, f32[4,36,16,128]{3,2,1,0:T(8,128)}, f32[3,36,16,128]{3,2,1,0:T(8,128)}, f32[3,36,16,128]{3,2,1,0:T(8,128)}) custom-call(s32[6]{0:T(128)} %stack.35.scalars, f32[4,36,32,512]{3,2,1,0:T(8,128)} %bitcast.12, s32[32,512]{1,0:T(8,128)} %mask_ref.13), custom_call_target="tpu_custom_call" | custom-call | tf_op jit(solution)/shard_map/pallas_call | solution.py:89
  36.8 2.5 collective-permute-done.20.other_ref.refs_1_
  39.3 0.6 collective-permute-start
  39.8 4.6 %collective-permute-done.15.refs_2_ = f32[3,36,16,128]{3,2,1,0:T(8,128)} collective-permute-done((f32[3,36,16,128]{3,2,1,0:T(8,128)}, f32[3,36,16,128]{3,2,1,0:T(8,128)}, u32[]{:S(2)}, u32[]{:S(2)}) %collective-permute-start.15) | collective-permute-done | bytes 884768 | tf_op jit(solution)/shard_map/ppermute | solution.py:569
  44.5 2.2 collective-permute-start.11
  47.0 16.5 %collective-permute-done.9.refs_2_ = f32[3,36,16,128]{3,2,1,0:T(8,128)} collective-permute-done((f32[3,36,16,128]{3,2,1,0:T(8,128)}, f32[3,36,16,128]{3,2,1,0:T(8,128)}, u32[]{:S(2)}, u32[]{:S(2)}) %collective-permute-start.9) | collective-permute-done | bytes 884768 | tf_op jit(solution)/shard_map/ppermute | solution.py:569
  63.4 2.1 collective-permute-start.3
  65.5 3.0 shard_map.113
  69.0 0.6 copy-done.2
  69.6 3.8 %shard_map.104 = (f32[4,36,16,128]{3,2,1,0:T(8,128)}, f32[4,36,16,128]{3,2,1,0:T(8,128)}) custom-call(s32[6]{0:T(128)} %stack.35.scalars, f32[4,36,16,128]{3,2,1,0:T(8,128)} %get-tuple-element.55.own_ref.refs_0_, f32[4,36,16,128]{3,2,1,0:T(8,128)} %copy-done.2), custom_call_target="tpu_custom_call" | custom-call | tf_op jit(solution)/shard_map/pallas_call | solution.py:133
  73.4 1.7 collective-permute-start.14
  75.1 7.3 %collective-permute-done.1.refs_2_ = f32[3,36,16,128]{3,2,1,0:T(8,128)} collective-permute-done((f32[3,36,16,128]{3,2,1,0:T(8,128)}, f32[3,36,16,128]{3,2,1,0:T(8,128)}, u32[]{:S(2)}, u32[]{:S(2)}) %collective-permute-start.1) | collective-permute-done | bytes 884768 | tf_op jit(solution)/shard_map/ppermute | solution.py:569
  82.4 1.2 collective-permute-start.10
  83.6 6.3 %collective-permute-done.other_ref.refs_1_ = f32[4,36,16,128]{3,2,1,0:T(8,128)S(1)} collective-permute-done((f32[4,36,16,128]{3,2,1,0:T(8,128)}, f32[4,36,16,128]{3,2,1,0:T(8,128)S(1)}, u32[]{:S(2)}, u32[]{:S(2)}) %collective-permute-start) | collective-permute-done | bytes 1179680 | tf_op jit(solution)/shard_map/ppermute | solution.py:563
  89.8 5.4 %collective-permute-start.12 = (f32[4,36,16,128]{3,2,1,0:T(8,128)}, f32[4,36,16,128]{3,2,1,0:T(8,128)}, u32[]{:S(2)}, u32[]{:S(2)}) collective-permute-start(f32[4,36,16,128]{3,2,1,0:T(8,128)} %get-tuple-element.60), channel_id=1, source_target_pairs={{0,8},{1,9},{2,4},{3,5},{4,2},{5,3},{6,14},{7,15},{8,0},{9,1},{10,... | collective-permute-start | bytes 3538952 | tf_op jit(solution)/shard_map/ppermute | solution.py:570
  95.3 3.7 %shard_map.101 = (f32[4,36,16,128]{3,2,1,0:T(8,128)}, f32[4,36,16,128]{3,2,1,0:T(8,128)}) custom-call(s32[6]{0:T(128)} %stack.35.scalars, f32[4,36,16,128]{3,2,1,0:T(8,128)} %get-tuple-element.47.own_ref.refs_0_, f32[4,36,16,128]{3,2,1,0:T(8,128)} %copy-done.1), custom_call_target="tpu_custom_call" | custom-call | tf_op jit(solution)/shard_map/pallas_call | solution.py:133
  99.1 3.6 %collective-permute-start.4 = (f32[4,36,16,128]{3,2,1,0:T(8,128)}, f32[4,36,16,128]{3,2,1,0:T(8,128)}, u32[]{:S(2)}, u32[]{:S(2)}) collective-permute-start(f32[4,36,16,128]{3,2,1,0:T(8,128)} %get-tuple-element.52), channel_id=1, source_target_pairs={{0,8},{1,9},{2,4},{3,5},{4,2},{5,3},{6,14},{7,15},{8,0},{9,1},{10,... | collective-permute-start | bytes 3538952 | tf_op jit(solution)/shard_map/ppermute | solution.py:570
  102.6 3.0 shard_map.110
  105.7 9.4 %collective-permute-done.14.other_ref.refs_1_ = f32[4,36,16,128]{3,2,1,0:T(8,128)S(1)} collective-permute-done((f32[4,36,16,128]{3,2,1,0:T(8,128)}, f32[4,36,16,128]{3,2,1,0:T(8,128)S(1)}, u32[]{:S(2)}, u32[]{:S(2)}) %collective-permute-start.14) | collective-permute-done | bytes 1179680 | tf_op jit(solution)/shard_map/ppermute | solution.py:563
  115.0 0.7 collective-permute-start.22
  115.7 4.5 %collective-permute-done.10.refs_3_ = f32[4,36,16,128]{3,2,1,0:T(8,128)S(1)} collective-permute-done((f32[4,36,16,128]{3,2,1,0:T(8,128)}, f32[4,36,16,128]{3,2,1,0:T(8,128)S(1)}, u32[]{:S(2)}, u32[]{:S(2)}) %collective-permute-start.10) | collective-permute-done | bytes 1179680 | tf_op jit(solution)/shard_map/ppermute | solution.py:570
  120.2 2.1 collective-permute-start.24
  122.3 3.7 %shard_map.107 = (f32[4,36,16,128]{3,2,1,0:T(8,128)}, f32[4,36,16,128]{3,2,1,0:T(8,128)}) custom-call(s32[6]{0:T(128)} %stack.35.scalars, f32[4,36,16,128]{3,2,1,0:T(8,128)} %get-tuple-element.63.own_ref.refs_0_, f32[4,36,16,128]{3,2,1,0:T(8,128)} %copy-done), custom_call_target="tpu_custom_call" | custom-call | tf_op jit(solution)/shard_map/pallas_call | solution.py:133
  126.0 0.5 collective-permute-start.16
  126.6 18.9 %collective-permute-done.2.refs_3_ = f32[4,36,16,128]{3,2,1,0:T(8,128)S(1)} collective-permute-done((f32[4,36,16,128]{3,2,1,0:T(8,128)}, f32[4,36,16,128]{3,2,1,0:T(8,128)S(1)}, u32[]{:S(2)}, u32[]{:S(2)}) %collective-permute-start.2) | collective-permute-done | bytes 1179680 | tf_op jit(solution)/shard_map/ppermute | solution.py:570
  145.5 2.1 collective-permute-start.18
  147.6 1.8 sine_multiply_fusion
  149.4 11.6 %shard_map.105 = (f32[4,36,16,128]{3,2,1,0:T(8,128)}, f32[4,36,16,128]{3,2,1,0:T(8,128)}) custom-call(s32[6]{0:T(128)} %stack.35.scalars, f32[32]{0:T(128)} %constant.33.clone.gain_ref, f32[32]{0:T(128)} %constant.34.clone.drop_ref, f32[32,512]{1,0:T(8,128)} %get-tuple-element.90.along_ref, f32[32,512]{1,0:T(8,128)} %get-tuple-element.89.across_ref, ...), custom_call_target="tpu_custom_call" | custom-call | tf_op jit(solution)/shard_map/pallas_call | solution.py:307
  161.2 11.5 %shard_map.102 = (f32[4,36,16,128]{3,2,1,0:T(8,128)}, f32[4,36,16,128]{3,2,1,0:T(8,128)}) custom-call(s32[6]{0:T(128)} %stack.35.scalars, f32[32]{0:T(128)} %constant.33.clone.gain_ref, f32[32]{0:T(128)} %constant.34.clone.drop_ref, f32[32,512]{1,0:T(8,128)} %get-tuple-element.90.along_ref, f32[32,512]{1,0:T(8,128)} %get-tuple-element.89.across_ref, ...), custom_call_target="tpu_custom_call" | custom-call | tf_op jit(solution)/shard_map/pallas_call | solution.py:307
  172.7 1.8 collective-permute-start.13
  174.5 7.5 %shard_map.111 = (f32[4,36,8,128]{3,2,1,0:T(8,128)}, f32[4,36,8,128]{3,2,1,0:T(8,128)}) custom-call(s32[6]{0:T(128)} %stack.35.scalars, f32[32]{0:T(128)} %constant.33.clone.gain_ref, f32[32]{0:T(128)} %constant.34.clone.drop_ref, f32[32,512]{1,0:T(8,128)} %get-tuple-element.90.along_ref, f32[32,512]{1,0:T(8,128)} %get-tuple-element.89.across_ref, ...), custom_call_target="tpu_custom_call" | custom-call | tf_op jit(solution)/shard_map/pallas_call | solution.py:307
  182.0 1.4 collective-permute-start.25
  183.5 7.5 %shard_map.114 = (f32[2,36,8,128]{3,2,1,0:T(8,128)}, f32[2,36,8,128]{3,2,1,0:T(8,128)}, f32[2,36,8,128]{3,2,1,0:T(8,128)}, f32[2,36,8,128]{3,2,1,0:T(8,128)}) custom-call(s32[6]{0:T(128)} %stack.35.scalars, f32[32]{0:T(128)} %constant.33.clone.gain_ref, f32[32]{0:T(128)} %constant.34.clone.drop_ref, f32[32,512]{1,0:T(8,128)} %get-tuple-element.90.along_ref, ...), custom_call_target="tpu_custom_call" | custom-call | tf_op jit(solution)/shard_map/pallas_call | solution.py:307
  191.0 1.0 copy-done.14
  192.0 0.7 collective-permute-start.34
  192.8 11.4 %shard_map.108 = (f32[4,36,16,128]{3,2,1,0:T(8,128)}, f32[4,36,16,128]{3,2,1,0:T(8,128)}) custom-call(s32[6]{0:T(128)} %stack.35.scalars, f32[32]{0:T(128)} %constant.33.clone.gain_ref, f32[32]{0:T(128)} %constant.34.clone.drop_ref, f32[32,512]{1,0:T(8,128)} %get-tuple-element.90.along_ref, f32[32,512]{1,0:T(8,128)} %get-tuple-element.89.across_ref, ...), custom_call_target="tpu_custom_call" | custom-call | tf_op jit(solution)/shard_map/pallas_call | solution.py:307
  204.2 0.8 collective-permute-start.19
  205.0 39.9 %collective-permute-done.34.refs_9_ = f32[2,36,8,128]{3,2,1,0:T(8,128)} collective-permute-done((f32[2,36,8,128]{3,2,1,0:T(8,128)}, f32[2,36,8,128]{3,2,1,0:T(8,128)}, u32[]{:S(2)}, u32[]{:S(2)}) %collective-permute-start.34) | collective-permute-done | bytes 294944 | tf_op jit(solution)/shard_map/ppermute | solution.py:583
  244.9 3.5 %collective-permute-start.32 = (f32[4,36,16,128]{3,2,1,0:T(8,128)S(1)}, f32[4,36,16,128]{3,2,1,0:T(8,128)S(1)}, u32[]{:S(2)}, u32[]{:S(2)}) collective-permute-start(f32[4,36,16,128]{3,2,1,0:T(8,128)S(1)} %copy-done.3), channel_id=1, source_target_pairs={{8,0},{16,8},{24,16},{9,1},{17,9},{25,17},{10,2},{18,10},{26,18},{... | collective-permute-start | bytes 3538952 | tf_op jit(solution)/shard_map/ppermute | solution.py:589
  248.4 3.5 %collective-permute-start.5 = (f32[4,36,16,128]{3,2,1,0:T(8,128)S(1)}, f32[4,36,16,128]{3,2,1,0:T(8,128)S(1)}, u32[]{:S(2)}, u32[]{:S(2)}) collective-permute-start(f32[4,36,16,128]{3,2,1,0:T(8,128)S(1)} %copy-done.4), channel_id=1, source_target_pairs={{0,8},{8,16},{16,24},{1,9},{9,17},{17,25},{2,10},{10,18},{18,26},{... | collective-permute-start | bytes 3538952 | tf_op jit(solution)/shard_map/ppermute | solution.py:589
  251.9 1.9 collective-permute-start.33
  253.9 3.8 %collective-permute-start.7 = (f32[4,36,16,128]{3,2,1,0:T(8,128)}, f32[4,36,16,128]{3,2,1,0:T(8,128)S(1)}, u32[]{:S(2)}, u32[]{:S(2)}) collective-permute-start(f32[4,36,16,128]{3,2,1,0:T(8,128)} %collective-permute-done.6.refs_11_), channel_id=1, source_target_pairs={{0,8},{8,16},{16,24},{1,9},{9,17},{17,25},{2,10},{10,18},{18,26},{... | collective-permute-start | bytes 3538952 | tf_op jit(solution)/shard_map/ppermute | solution.py:589
  257.7 12.4 %collective-permute-done.19.refs_5_ = f32[4,36,16,128]{3,2,1,0:T(8,128)S(1)} collective-permute-done((f32[4,36,16,128]{3,2,1,0:T(8,128)}, f32[4,36,16,128]{3,2,1,0:T(8,128)S(1)}, u32[]{:S(2)}, u32[]{:S(2)}) %collective-permute-start.19) | collective-permute-done | bytes 1179680 | tf_op jit(solution)/shard_map/ppermute | solution.py:583
  270.1 1.2 collective-permute-start.31
  271.3 5.5 %collective-permute-done.33.refs_13_ = f32[4,36,16,128]{3,2,1,0:T(8,128)S(1)} collective-permute-done((f32[4,36,16,128]{3,2,1,0:T(8,128)S(1)}, f32[4,36,16,128]{3,2,1,0:T(8,128)S(1)}, u32[]{:S(2)}, u32[]{:S(2)}) %collective-permute-start.33) | collective-permute-done | bytes 1179680 | tf_op jit(solution)/shard_map/ppermute | solution.py:589
  276.9 0.9 collective-permute-done.7.refs_1_
  277.9 0.9 copy-done.10
  278.8 14.5 %shard_map.115.refs_14_ = f32[4,36,32,512]{3,2,1,0:T(8,128)} custom-call(s32[6]{0:T(128)} %stack.35.scalars, f32[32]{0:T(128)} %constant.35.clone.speed_ref, f32[36]{0:T(128)} %constant.36.clone.cos_ref, f32[36]{0:T(128)} %constant.37.clone.sin_ref, f32[3,32,128]{2,1,0:T(8,128)} %constant.38.clone.geo_ref, s32[32,512]{1,0:T(8,128)} %mask_ref.13, ...), custom_call_target="tpu_custom_call" | custom-call | tf_op jit(solution)/shard_map/pallas_call | solution.py:448
  293.3 14.6 %shard_map.116 = f32[4,36,32,512]{3,2,1,0:T(8,128)} custom-call(s32[6]{0:T(128)} %stack.35.scalars, f32[32]{0:T(128)} %constant.35.clone.speed_ref, f32[36]{0:T(128)} %constant.36.clone.cos_ref, f32[36]{0:T(128)} %constant.37.clone.sin_ref, f32[3,32,128]{2,1,0:T(8,128)} %constant.38.clone.geo_ref, ...), custom_call_target="tpu_custom_call", output_to_operand_aliasing={{}: (20, {})} | custom-call | tf_op jit(solution)/shard_map/pallas_call | solution.py:448
  (73 shorter events, 1.7 us)
Async XLA Ops:
  3.7 14.6 %collective-permute-start.27 = (f32[3,36,8,128]{3,2,1,0:T(8,128)}, f32[3,36,8,128]{3,2,1,0:T(8,128)S(1)}, u32[]{:S(2)}, u32[]{:S(2)}) collective-permute-start(f32[3,36,8,128]{3,2,1,0:T(8,128)} %get-tuple-element.81), channel_id=1, source_target_pairs={{0,2},{1,3},{2,0},{3,1},{4,6},{5,7},{6,4},{7,5},{8,10},{9,11},{10,... | collective-permute-start | bytes 1327112 | tf_op jit(solution)/shard_map/ppermute | solution.py:569
  5.8 7.3 %copy-start.23 = (f32[4,36,8,128]{3,2,1,0:T(8,128)S(1)}, f32[4,36,8,128]{3,2,1,0:T(8,128)}, u32[]{:S(2)}) copy-start(f32[4,36,8,128]{3,2,1,0:T(8,128)} %get-tuple-element.80) | copy-start | bytes 1769476
  5.8 12.6 %collective-permute-start.29 = (f32[3,36,8,128]{3,2,1,0:T(8,128)}, f32[3,36,8,128]{3,2,1,0:T(8,128)S(1)}, u32[]{:S(2)}, u32[]{:S(2)}) collective-permute-start(f32[3,36,8,128]{3,2,1,0:T(8,128)} %get-tuple-element.83), channel_id=1, source_target_pairs={{0,8},{1,9},{2,4},{3,5},{4,2},{5,3},{6,14},{7,15},{8,0},{9,1},{10,... | collective-permute-start | bytes 1327112 | tf_op jit(solution)/shard_map/ppermute | solution.py:569
  9.9 15.5 %collective-permute-start.21 = (f32[3,36,8,128]{3,2,1,0:T(8,128)}, f32[3,36,8,128]{3,2,1,0:T(8,128)S(1)}, u32[]{:S(2)}, u32[]{:S(2)}) collective-permute-start(f32[3,36,8,128]{3,2,1,0:T(8,128)} %get-tuple-element.73), channel_id=1, source_target_pairs={{0,2},{1,3},{2,0},{3,1},{4,6},{5,7},{6,4},{7,5},{8,10},{9,11},{10,... | collective-permute-start | bytes 1327112 | tf_op jit(solution)/shard_map/ppermute | solution.py:569
  11.6 19.7 %collective-permute-start.23 = (f32[3,36,8,128]{3,2,1,0:T(8,128)}, f32[3,36,8,128]{3,2,1,0:T(8,128)S(1)}, u32[]{:S(2)}, u32[]{:S(2)}) collective-permute-start(f32[3,36,8,128]{3,2,1,0:T(8,128)} %get-tuple-element.75), channel_id=1, source_target_pairs={{0,8},{1,9},{2,4},{3,5},{4,2},{5,3},{6,14},{7,15},{8,0},{9,1},{10,... | collective-permute-start | bytes 1327112 | tf_op jit(solution)/shard_map/ppermute | solution.py:569
  13.1 19.5 %collective-permute-start.26 = (f32[4,36,8,128]{3,2,1,0:T(8,128)S(1)}, f32[4,36,8,128]{3,2,1,0:T(8,128)S(1)}, u32[]{:S(2)}, u32[]{:S(2)}) collective-permute-start(f32[4,36,8,128]{3,2,1,0:T(8,128)S(1)} %copy-done.23), channel_id=1, source_target_pairs={{0,1},{1,0},{2,3},{3,2},{4,5},{5,4},{6,7},{7,6},{8,9},{9,8},{10,11... | collective-permute-start | bytes 1769480 | tf_op jit(solution)/shard_map/ppermute | solution.py:563
  18.3 12.9 %copy-start.18 = (f32[3,36,8,128]{3,2,1,0:T(8,128)}, f32[3,36,8,128]{3,2,1,0:T(8,128)S(1)}, u32[]{:S(2)}) copy-start(f32[3,36,8,128]{3,2,1,0:T(8,128)S(1)} %collective-permute-done.27.refs_2_) | copy-start | bytes 1327108
  18.3 26.1 %collective-permute-start.15 = (f32[3,36,16,128]{3,2,1,0:T(8,128)}, f32[3,36,16,128]{3,2,1,0:T(8,128)}, u32[]{:S(2)}, u32[]{:S(2)}) collective-permute-start(f32[3,36,16,128]{3,2,1,0:T(8,128)} %get-tuple-element.65), channel_id=1, source_target_pairs={{0,2},{1,3},{2,0},{3,1},{4,6},{5,7},{6,4},{7,5},{8,10},{9,11},{10,... | collective-permute-start | bytes 2654216 | tf_op jit(solution)/shard_map/ppermute | solution.py:569
  18.4 7.0 %copy-start.19 = (f32[3,36,8,128]{3,2,1,0:T(8,128)}, f32[3,36,8,128]{3,2,1,0:T(8,128)S(1)}, u32[]{:S(2)}) copy-start(f32[3,36,8,128]{3,2,1,0:T(8,128)S(1)} %collective-permute-done.29.refs_4_) | copy-start | bytes 1327108
  18.4 28.2 %collective-permute-start.17 = (f32[3,36,16,128]{3,2,1,0:T(8,128)}, f32[3,36,16,128]{3,2,1,0:T(8,128)}, u32[]{:S(2)}, u32[]{:S(2)}) collective-permute-start(f32[3,36,16,128]{3,2,1,0:T(8,128)} %get-tuple-element.67), channel_id=1, source_target_pairs={{0,8},{1,9},{2,4},{3,5},{4,2},{5,3},{6,14},{7,15},{8,0},{9,1},{10,... | collective-permute-start | bytes 2654216 | tf_op jit(solution)/shard_map/ppermute | solution.py:569
  25.4 0.8 copy-start.20
  26.2 13.1 %collective-permute-start.20 = (f32[4,36,8,128]{3,2,1,0:T(8,128)}, f32[4,36,8,128]{3,2,1,0:T(8,128)S(1)}, u32[]{:S(2)}, u32[]{:S(2)}) collective-permute-start(f32[4,36,8,128]{3,2,1,0:T(8,128)} %get-tuple-element.72), channel_id=1, source_target_pairs={{0,1},{1,0},{2,3},{3,2},{4,5},{5,4},{6,7},{7,6},{8,9},{9,8},{10,11... | collective-permute-start | bytes 1769480 | tf_op jit(solution)/shard_map/ppermute | solution.py:563
  31.2 5.6 %copy-start.21 = (f32[3,36,8,128]{3,2,1,0:T(8,128)}, f32[3,36,8,128]{3,2,1,0:T(8,128)S(1)}, u32[]{:S(2)}) copy-start(f32[3,36,8,128]{3,2,1,0:T(8,128)S(1)} %collective-permute-done.23.refs_4_) | copy-start | bytes 1327108
  31.3 32.2 %collective-permute-start.9 = (f32[3,36,16,128]{3,2,1,0:T(8,128)}, f32[3,36,16,128]{3,2,1,0:T(8,128)}, u32[]{:S(2)}, u32[]{:S(2)}) collective-permute-start(f32[3,36,16,128]{3,2,1,0:T(8,128)} %get-tuple-element.57), channel_id=1, source_target_pairs={{0,2},{1,3},{2,0},{3,1},{4,6},{5,7},{6,4},{7,5},{8,10},{9,11},{10,... | collective-permute-start | bytes 2654216 | tf_op jit(solution)/shard_map/ppermute | solution.py:569
  32.6 4.2 %copy-start.11 = (f32[4,36,8,128]{3,2,1,0:T(8,128)}, f32[4,36,8,128]{3,2,1,0:T(8,128)S(1)}, u32[]{:S(2)}) copy-start(f32[4,36,8,128]{3,2,1,0:T(8,128)S(1)} %collective-permute-done.26.other_ref.refs_1_) | copy-start | bytes 1769476
  32.6 35.9 %collective-permute-start.8 = (f32[4,36,16,128]{3,2,1,0:T(8,128)}, f32[4,36,16,128]{3,2,1,0:T(8,128)S(1)}, u32[]{:S(2)}, u32[]{:S(2)}) collective-permute-start(f32[4,36,16,128]{3,2,1,0:T(8,128)} %get-tuple-element.56), channel_id=1, source_target_pairs={{0,1},{1,0},{2,3},{3,2},{4,5},{5,4},{6,7},{7,6},{8,9},{9,8},{10,11... | collective-permute-start | bytes 3538952 | tf_op jit(solution)/shard_map/ppermute | solution.py:563
  39.3 34.1 %copy-start.12 = (f32[4,36,8,128]{3,2,1,0:T(8,128)}, f32[4,36,8,128]{3,2,1,0:T(8,128)S(1)}, u32[]{:S(2)}) copy-start(f32[4,36,8,128]{3,2,1,0:T(8,128)S(1)} %collective-permute-done.20.other_ref.refs_1_) | copy-start | bytes 1769476
  39.3 50.6 %collective-permute-start = (f32[4,36,16,128]{3,2,1,0:T(8,128)}, f32[4,36,16,128]{3,2,1,0:T(8,128)S(1)}, u32[]{:S(2)}, u32[]{:S(2)}) collective-permute-start(f32[4,36,16,128]{3,2,1,0:T(8,128)} %get-tuple-element.48), channel_id=1, source_target_pairs={{0,1},{1,0},{2,3},{3,2},{4,5},{5,4},{6,7},{7,6},{8,9},{9,8},{10,11... | collective-permute-start | bytes 3538952 | tf_op jit(solution)/shard_map/ppermute | solution.py:563
  44.5 28.9 %collective-permute-start.11 = (f32[3,36,16,128]{3,2,1,0:T(8,128)}, f32[3,36,16,128]{3,2,1,0:T(8,128)}, u32[]{:S(2)}, u32[]{:S(2)}) collective-permute-start(f32[3,36,16,128]{3,2,1,0:T(8,128)} %get-tuple-element.59), channel_id=1, source_target_pairs={{0,8},{1,9},{2,4},{3,5},{4,2},{5,3},{6,14},{7,15},{8,0},{9,1},{10,... | collective-permute-start | bytes 2654216 | tf_op jit(solution)/shard_map/ppermute | solution.py:569
  46.7 35.7 %collective-permute-start.1 = (f32[3,36,16,128]{3,2,1,0:T(8,128)}, f32[3,36,16,128]{3,2,1,0:T(8,128)}, u32[]{:S(2)}, u32[]{:S(2)}) collective-permute-start(f32[3,36,16,128]{3,2,1,0:T(8,128)} %get-tuple-element.49), channel_id=1, source_target_pairs={{0,2},{1,3},{2,0},{3,1},{4,6},{5,7},{6,4},{7,5},{8,10},{9,11},{10,... | collective-permute-start | bytes 2654216 | tf_op jit(solution)/shard_map/ppermute | solution.py:569
  63.4 35.5 %collective-permute-start.3 = (f32[3,36,16,128]{3,2,1,0:T(8,128)}, f32[3,36,16,128]{3,2,1,0:T(8,128)}, u32[]{:S(2)}, u32[]{:S(2)}) collective-permute-start(f32[3,36,16,128]{3,2,1,0:T(8,128)} %get-tuple-element.51), channel_id=1, source_target_pairs={{0,8},{1,9},{2,4},{3,5},{4,2},{5,3},{6,14},{7,15},{8,0},{9,1},{10,... | collective-permute-start | bytes 2654216 | tf_op jit(solution)/shard_map/ppermute | solution.py:569
  68.5 1.1 copy-start.2
  68.5 30.5 %collective-permute-start.28 = (f32[4,36,8,128]{3,2,1,0:T(8,128)}, f32[4,36,8,128]{3,2,1,0:T(8,128)}, u32[]{:S(2)}, u32[]{:S(2)}) collective-permute-start(f32[4,36,8,128]{3,2,1,0:T(8,128)} %get-tuple-element.82), channel_id=1, source_target_pairs={{0,2},{1,3},{2,0},{3,1},{4,6},{5,7},{6,4},{7,5},{8,10},{9,11},{10,... | collective-permute-start | bytes 1769480 | tf_op jit(solution)/shard_map/ppermute | solution.py:570
  73.4 41.6 %collective-permute-start.14 = (f32[4,36,16,128]{3,2,1,0:T(8,128)}, f32[4,36,16,128]{3,2,1,0:T(8,128)S(1)}, u32[]{:S(2)}, u32[]{:S(2)}) collective-permute-start(f32[4,36,16,128]{3,2,1,0:T(8,128)} %get-tuple-element.64), channel_id=1, source_target_pairs={{0,1},{1,0},{2,3},{3,2},{4,5},{5,4},{6,7},{7,6},{8,9},{9,8},{10,11... | collective-permute-start | bytes 3538952 | tf_op jit(solution)/shard_map/ppermute | solution.py:563
  82.4 37.8 %collective-permute-start.10 = (f32[4,36,16,128]{3,2,1,0:T(8,128)}, f32[4,36,16,128]{3,2,1,0:T(8,128)S(1)}, u32[]{:S(2)}, u32[]{:S(2)}) collective-permute-start(f32[4,36,16,128]{3,2,1,0:T(8,128)} %get-tuple-element.58), channel_id=1, source_target_pairs={{0,2},{1,3},{2,0},{3,1},{4,6},{5,7},{6,4},{7,5},{8,10},{9,11},{10,... | collective-permute-start | bytes 3538952 | tf_op jit(solution)/shard_map/ppermute | solution.py:570
  89.8 5.4 %copy-start.1 = (f32[4,36,16,128]{3,2,1,0:T(8,128)}, f32[4,36,16,128]{3,2,1,0:T(8,128)S(1)}, u32[]{:S(2)}) copy-start(f32[4,36,16,128]{3,2,1,0:T(8,128)S(1)} %collective-permute-done.other_ref.refs_1_) | copy-start | bytes 3538948
  89.8 36.2 %collective-permute-start.12 = (f32[4,36,16,128]{3,2,1,0:T(8,128)}, f32[4,36,16,128]{3,2,1,0:T(8,128)}, u32[]{:S(2)}, u32[]{:S(2)}) collective-permute-start(f32[4,36,16,128]{3,2,1,0:T(8,128)} %get-tuple-element.60), channel_id=1, source_target_pairs={{0,8},{1,9},{2,4},{3,5},{4,2},{5,3},{6,14},{7,15},{8,0},{9,1},{10,... | collective-permute-start | bytes 3538952 | tf_op jit(solution)/shard_map/ppermute | solution.py:570
  99.0 46.5 %collective-permute-start.2 = (f32[4,36,16,128]{3,2,1,0:T(8,128)}, f32[4,36,16,128]{3,2,1,0:T(8,128)S(1)}, u32[]{:S(2)}, u32[]{:S(2)}) collective-permute-start(f32[4,36,16,128]{3,2,1,0:T(8,128)} %get-tuple-element.50), channel_id=1, source_target_pairs={{0,2},{1,3},{2,0},{3,1},{4,6},{5,7},{6,4},{7,5},{8,10},{9,11},{10,... | collective-permute-start | bytes 3538952 | tf_op jit(solution)/shard_map/ppermute | solution.py:570
  99.1 61.9 %collective-permute-start.4 = (f32[4,36,16,128]{3,2,1,0:T(8,128)}, f32[4,36,16,128]{3,2,1,0:T(8,128)}, u32[]{:S(2)}, u32[]{:S(2)}) collective-permute-start(f32[4,36,16,128]{3,2,1,0:T(8,128)} %get-tuple-element.52), channel_id=1, source_target_pairs={{0,8},{1,9},{2,4},{3,5},{4,2},{5,3},{6,14},{7,15},{8,0},{9,1},{10,... | collective-permute-start | bytes 3538952 | tf_op jit(solution)/shard_map/ppermute | solution.py:570
  115.0 7.3 %copy-start = (f32[4,36,16,128]{3,2,1,0:T(8,128)}, f32[4,36,16,128]{3,2,1,0:T(8,128)S(1)}, u32[]{:S(2)}) copy-start(f32[4,36,16,128]{3,2,1,0:T(8,128)S(1)} %collective-permute-done.14.other_ref.refs_1_) | copy-start | bytes 3538948
  115.0 57.6 %collective-permute-start.22 = (f32[4,36,8,128]{3,2,1,0:T(8,128)}, f32[4,36,8,128]{3,2,1,0:T(8,128)}, u32[]{:S(2)}, u32[]{:S(2)}) collective-permute-start(f32[4,36,8,128]{3,2,1,0:T(8,128)} %get-tuple-element.74), channel_id=1, source_target_pairs={{0,2},{1,3},{2,0},{3,1},{4,6},{5,7},{6,4},{7,5},{8,10},{9,11},{10,... | collective-permute-start | bytes 1769480 | tf_op jit(solution)/shard_map/ppermute | solution.py:570
  120.2 5.8 %copy-start.15 = (f32[4,36,16,128]{3,2,1,0:T(8,128)}, f32[4,36,16,128]{3,2,1,0:T(8,128)S(1)}, u32[]{:S(2)}) copy-start(f32[4,36,16,128]{3,2,1,0:T(8,128)S(1)} %collective-permute-done.10.refs_3_) | copy-start | bytes 3538948
  120.2 54.2 %collective-permute-start.24 = (f32[4,36,8,128]{3,2,1,0:T(8,128)}, f32[4,36,8,128]{3,2,1,0:T(8,128)}, u32[]{:S(2)}, u32[]{:S(2)}) collective-permute-start(f32[4,36,8,128]{3,2,1,0:T(8,128)} %get-tuple-element.76), channel_id=1, source_target_pairs={{0,8},{1,9},{2,4},{3,5},{4,2},{5,3},{6,14},{7,15},{8,0},{9,1},{10,... | collective-permute-start | bytes 1769480 | tf_op jit(solution)/shard_map/ppermute | solution.py:570
  126.0 65.0 %collective-permute-start.16 = (f32[4,36,16,128]{3,2,1,0:T(8,128)}, f32[4,36,16,128]{3,2,1,0:T(8,128)S(1)}, u32[]{:S(2)}, u32[]{:S(2)}) collective-permute-start(f32[4,36,16,128]{3,2,1,0:T(8,128)} %get-tuple-element.66), channel_id=1, source_target_pairs={{0,2},{1,3},{2,0},{3,1},{4,6},{5,7},{6,4},{7,5},{8,10},{9,11},{10,... | collective-permute-start | bytes 3538952 | tf_op jit(solution)/shard_map/ppermute | solution.py:570
  145.5 15.5 %copy-start.16 = (f32[4,36,16,128]{3,2,1,0:T(8,128)}, f32[4,36,16,128]{3,2,1,0:T(8,128)S(1)}, u32[]{:S(2)}) copy-start(f32[4,36,16,128]{3,2,1,0:T(8,128)S(1)} %collective-permute-done.2.refs_3_) | copy-start | bytes 3538948
  145.5 47.3 %collective-permute-start.18 = (f32[4,36,16,128]{3,2,1,0:T(8,128)}, f32[4,36,16,128]{3,2,1,0:T(8,128)}, u32[]{:S(2)}, u32[]{:S(2)}) collective-permute-start(f32[4,36,16,128]{3,2,1,0:T(8,128)} %get-tuple-element.68), channel_id=1, source_target_pairs={{0,8},{1,9},{2,4},{3,5},{4,2},{5,3},{6,14},{7,15},{8,0},{9,1},{10,... | collective-permute-start | bytes 3538952 | tf_op jit(solution)/shard_map/ppermute | solution.py:570
  149.4 11.6 %copy-start.22 = (f32[4,36,8,128]{3,2,1,0:T(8,128)S(1)}, f32[4,36,8,128]{3,2,1,0:T(8,128)}, u32[]{:S(2)}) copy-start(f32[4,36,8,128]{3,2,1,0:T(8,128)} %get-tuple-element.84) | copy-start | bytes 1769476
  161.0 21.0 %collective-permute-start.30 = (f32[4,36,8,128]{3,2,1,0:T(8,128)S(1)}, f32[4,36,8,128]{3,2,1,0:T(8,128)S(1)}, u32[]{:S(2)}, u32[]{:S(2)}) collective-permute-start(f32[4,36,8,128]{3,2,1,0:T(8,128)S(1)} %copy-done.22), channel_id=1, source_target_pairs={{0,8},{1,9},{2,4},{3,5},{4,2},{5,3},{6,14},{7,15},{8,0},{9,1},{10,... | collective-permute-start | bytes 1769480 | tf_op jit(solution)/shard_map/ppermute | solution.py:570
  172.7 79.2 %collective-permute-start.13 = (f32[4,36,16,128]{3,2,1,0:T(8,128)}, f32[4,36,16,128]{3,2,1,0:T(8,128)S(1)}, u32[]{:S(2)}, u32[]{:S(2)}) collective-permute-start(f32[4,36,16,128]{3,2,1,0:T(8,128)} %get-tuple-element.62), channel_id=1, source_target_pairs={{1,0},{0,1},{3,2},{2,3},{5,4},{4,5},{7,6},{6,7},{9,8},{8,9},{11,10... | collective-permute-start | bytes 3538952 | tf_op jit(solution)/shard_map/ppermute | solution.py:583
  174.4 79.4 %collective-permute-start.6 = (f32[4,36,16,128]{3,2,1,0:T(8,128)}, f32[4,36,16,128]{3,2,1,0:T(8,128)}, u32[]{:S(2)}, u32[]{:S(2)}) collective-permute-start(f32[4,36,16,128]{3,2,1,0:T(8,128)} %get-tuple-element.54), channel_id=1, source_target_pairs={{1,0},{0,1},{3,2},{2,3},{5,4},{4,5},{7,6},{6,7},{9,8},{8,9},{11,10... | collective-permute-start | bytes 3538952 | tf_op jit(solution)/shard_map/ppermute | solution.py:583
  182.0 1.5 copy-start.17
  182.0 66.4 %collective-permute-start.25 = (f32[4,36,8,128]{3,2,1,0:T(8,128)}, f32[4,36,8,128]{3,2,1,0:T(8,128)S(1)}, u32[]{:S(2)}, u32[]{:S(2)}) collective-permute-start(f32[4,36,8,128]{3,2,1,0:T(8,128)} %get-tuple-element.78), channel_id=1, source_target_pairs={{1,0},{0,1},{3,2},{2,3},{5,4},{4,5},{7,6},{6,7},{9,8},{8,9},{11,10... | collective-permute-start | bytes 1769480 | tf_op jit(solution)/shard_map/ppermute | solution.py:583
  191.0 1.0 copy-start.14
  192.0 52.9 %copy-start.3 = (f32[4,36,16,128]{3,2,1,0:T(8,128)S(1)}, f32[4,36,16,128]{3,2,1,0:T(8,128)}, u32[]{:S(2)}) copy-start(f32[4,36,16,128]{3,2,1,0:T(8,128)} %get-tuple-element.61.refs_2_) | copy-start | bytes 3538948
  192.0 56.4 %copy-start.4 = (f32[4,36,16,128]{3,2,1,0:T(8,128)S(1)}, f32[4,36,16,128]{3,2,1,0:T(8,128)}, u32[]{:S(2)}) copy-start(f32[4,36,16,128]{3,2,1,0:T(8,128)} %get-tuple-element.53.refs_10_) | copy-start | bytes 3538948
  192.0 52.9 %collective-permute-start.34 = (f32[2,36,8,128]{3,2,1,0:T(8,128)}, f32[2,36,8,128]{3,2,1,0:T(8,128)}, u32[]{:S(2)}, u32[]{:S(2)}) collective-permute-start(f32[2,36,8,128]{3,2,1,0:T(8,128)} %get-tuple-element.88), channel_id=1, source_target_pairs={{1,0},{0,1},{3,2},{2,3},{5,4},{4,5},{7,6},{6,7},{9,8},{8,9},{11,10... | collective-permute-start | bytes 884744 | tf_op jit(solution)/shard_map/ppermute | solution.py:583
  204.2 65.9 %collective-permute-start.19 = (f32[4,36,16,128]{3,2,1,0:T(8,128)}, f32[4,36,16,128]{3,2,1,0:T(8,128)S(1)}, u32[]{:S(2)}, u32[]{:S(2)}) collective-permute-start(f32[4,36,16,128]{3,2,1,0:T(8,128)} %get-tuple-element.70), channel_id=1, source_target_pairs={{1,0},{0,1},{3,2},{2,3},{5,4},{4,5},{7,6},{6,7},{9,8},{8,9},{11,10... | collective-permute-start | bytes 3538952 | tf_op jit(solution)/shard_map/ppermute | solution.py:583
  244.9 26.4 %collective-permute-start.32 = (f32[4,36,16,128]{3,2,1,0:T(8,128)S(1)}, f32[4,36,16,128]{3,2,1,0:T(8,128)S(1)}, u32[]{:S(2)}, u32[]{:S(2)}) collective-permute-start(f32[4,36,16,128]{3,2,1,0:T(8,128)S(1)} %copy-done.3), channel_id=1, source_target_pairs={{8,0},{16,8},{24,16},{9,1},{17,9},{25,17},{10,2},{18,10},{26,18},{... | collective-permute-start | bytes 3538952 | tf_op jit(solution)/shard_map/ppermute | solution.py:589
  248.4 30.4 %copy-start.13 = (f32[4,36,8,128]{3,2,1,0:T(8,128)}, f32[4,36,8,128]{3,2,1,0:T(8,128)S(1)}, u32[]{:S(2)}) copy-start(f32[4,36,8,128]{3,2,1,0:T(8,128)S(1)} %collective-permute-done.25.refs_7_) | copy-start | bytes 1769476
  248.4 22.9 %collective-permute-start.5 = (f32[4,36,16,128]{3,2,1,0:T(8,128)S(1)}, f32[4,36,16,128]{3,2,1,0:T(8,128)S(1)}, u32[]{:S(2)}, u32[]{:S(2)}) collective-permute-start(f32[4,36,16,128]{3,2,1,0:T(8,128)S(1)} %copy-done.4), channel_id=1, source_target_pairs={{0,8},{8,16},{16,24},{1,9},{9,17},{17,25},{2,10},{10,18},{18,26},{... | collective-permute-start | bytes 3538952 | tf_op jit(solution)/shard_map/ppermute | solution.py:589
  251.9 26.9 %copy-start.5 = (f32[4,36,16,128]{3,2,1,0:T(8,128)}, f32[4,36,16,128]{3,2,1,0:T(8,128)S(1)}, u32[]{:S(2)}) copy-start(f32[4,36,16,128]{3,2,1,0:T(8,128)S(1)} %collective-permute-done.13.refs_3_) | copy-start | bytes 3538948
  251.9 24.9 %collective-permute-start.33 = (f32[4,36,16,128]{3,2,1,0:T(8,128)S(1)}, f32[4,36,16,128]{3,2,1,0:T(8,128)S(1)}, u32[]{:S(2)}, u32[]{:S(2)}) collective-permute-start(f32[4,36,16,128]{3,2,1,0:T(8,128)S(1)} %collective-permute-done.13.refs_3_), channel_id=1, source_target_pairs={{8,0},{16,8},{24,16},{9,1},{17,9},{25,17},{10,2},{18,10},{26,18},{... | collective-permute-start | bytes 3538952 | tf_op jit(solution)/shard_map/ppermute | solution.py:589
  253.9 23.9 %collective-permute-start.7 = (f32[4,36,16,128]{3,2,1,0:T(8,128)}, f32[4,36,16,128]{3,2,1,0:T(8,128)S(1)}, u32[]{:S(2)}, u32[]{:S(2)}) collective-permute-start(f32[4,36,16,128]{3,2,1,0:T(8,128)} %collective-permute-done.6.refs_11_), channel_id=1, source_target_pairs={{0,8},{8,16},{16,24},{1,9},{9,17},{17,25},{2,10},{10,18},{18,26},{... | collective-permute-start | bytes 3538952 | tf_op jit(solution)/shard_map/ppermute | solution.py:589
  270.1 6.8 %copy-start.6 = (f32[4,36,16,128]{3,2,1,0:T(8,128)}, f32[4,36,16,128]{3,2,1,0:T(8,128)S(1)}, u32[]{:S(2)}) copy-start(f32[4,36,16,128]{3,2,1,0:T(8,128)S(1)} %collective-permute-done.19.refs_5_) | copy-start | bytes 3538948
  270.1 23.2 %collective-permute-start.31 = (f32[2,36,8,128]{3,2,1,0:T(8,128)}, f32[2,36,8,128]{3,2,1,0:T(8,128)}, u32[]{:S(2)}, u32[]{:S(2)}) collective-permute-start(f32[2,36,8,128]{3,2,1,0:T(8,128)} %get-tuple-element.86), channel_id=1, source_target_pairs={{1,0},{0,1},{3,2},{2,3},{5,4},{4,5},{7,6},{6,7},{9,8},{8,9},{11,10... | collective-permute-start | bytes 884744 | tf_op jit(solution)/shard_map/ppermute | solution.py:583
  271.3 6.5 %copy-start.7 = (f32[4,36,16,128]{3,2,1,0:T(8,128)}, f32[4,36,16,128]{3,2,1,0:T(8,128)S(1)}, u32[]{:S(2)}) copy-start(f32[4,36,16,128]{3,2,1,0:T(8,128)S(1)} %collective-permute-done.32.refs_12_) | copy-start | bytes 3538948
  271.3 6.5 %copy-start.8 = (f32[4,36,16,128]{3,2,1,0:T(8,128)}, f32[4,36,16,128]{3,2,1,0:T(8,128)S(1)}, u32[]{:S(2)}) copy-start(f32[4,36,16,128]{3,2,1,0:T(8,128)S(1)} %collective-permute-done.5.refs_0_) | copy-start | bytes 3538948
  276.9 1.1 copy-start.9
  277.8 1.0 copy-start.10
where the time goes:
time: 310 us; the launch traced here: 308 us
  waiting for transfers between devices  134 us (43%)
  Pallas kernels  114 us (37%)
  starting transfers between devices  53.9 us (17%)
  local copies, waits for them, and re-layouts  4.1 us (1%)
    ppermute x6, waiting for transfers between devices, shards(): own = [lax.ppermute(value, 'comp', returns[turn]) for value in own]  52.3 us
    pallas_call x5, Pallas kernels, source(): pl.pallas_call(functools.partial(source_kernel, parts, freqs, dirs, rows,...  49.5 us
    ppermute x10, waiting for transfers between devices, shards(): operands.append(lax.ppermute(packed[parts + side], both, pairs))  33.7 us
    pallas_call x2, Pallas kernels, sweep(): pl.pallas_call(functools.partial(sweep_kernel, parts, [[None] * len(piece...  29.1 us
    ppermute x10, waiting for transfers between devices, shards(): operands.append(lax.ppermute(joined[side], both, pairs))  23.4 us
    pallas_call x5, Pallas kernels, pack(): pl.pallas_call(functools.partial(pack_kernel, parts, rows, low, size, lea...  18.1 us
    ppermute x5, waiting for transfers between devices, shards(): lax.ppermute(packed[turn], 'comp', turns[turn])  18.1 us
    pallas_call x5, Pallas kernels, join(): pl.pallas_call(functools.partial(join_kernel, own.shape[0]), out_shape=[s...  17.2 us
  transfers between devices with their start and end apart: 35, of which 13 were waited for; matrix products, arithmetic and copies ran while one was open for 1% of the time, Pallas kernels for 31%

commit v1 on v0

--- a/solution.py
+++ b/solution.py
@@ -64,13 +64,19 @@
 
 def pack_kernel(parts, rows, low, size, lean, scalars, x_ref, mask_ref, *outs):
     spot = scalars[SPOT]
-    mask = mask_ref[...].astype(jnp.float32)
-    starts = [b * rows + low for b in range(parts)]
     freqs = x_ref.shape[0]
-    for f in range(freqs):
-        blocks = [x_ref[f, :, s : s + size, :] * mask[None, s : s + size, :] for s in starts]
-        for turn in range(parts):
-            outs[turn][f] = pick(blocks, lax.rem(spot + turn, parts))
+    for turn in range(parts):
+        block = lax.rem(spot + turn, parts)
+        if size % 8 == 0:
+            here = pl.ds(pl.multiple_of(block * rows + low, 8), size)
+            mask = mask_ref[here].astype(jnp.float32)
+            for f in range(freqs):
+                outs[turn][f] = x_ref[f, :, here, :] * mask[None]
+        else:
+            spots = [slice(b * rows + low, b * rows + low + size) for b in range(parts)]
+            mask = pick([mask_ref[here] for here in spots], block).astype(jnp.float32)
+            for f in range(freqs):
+                outs[turn][f] = pick([x_ref[f, :, here, :] for here in spots], block) * mask[None]
     if lean:
         even = scalars[EVEN]
         outs[parts][...] = outs[0][pl.ds(even, freqs - 1)]
@@ -333,6 +339,18 @@
 
 
 EDGE = 8
+INVERSE, AHEAD, BEHIND, AHEAD_NOT_FIRST, BEHIND_NOT_FIRST, BEHIND_NOT_FIRST_TWO = range(6)
+AHEAD_NOT_LAST, BEHIND_NOT_LAST, AHEAD_NOT_LAST_TWO = range(6, 9)
+
+
+def cell_weights(courant):
+    def combine(forward):
+        low, mid, high = face_weights(courant, forward)
+        if forward:
+            return (low, mid - low, 1.0 - mid + high, -high)
+        return (low, 1.0 - low + mid, high - mid, -high)
+
+    return combine
 
 
 def sweep_kernel(parts, layout, dirs, rows, start, aliased, scalars, speed_ref, cos_ref, sin_ref,
@@ -340,90 +358,106 @@
     tiles = len(layout) - 2
     count = sum(len(pieces) for pieces in layout) * parts
     ins = refs[:count]
-    out_ref, buffer = refs[count + aliased :]
+    out_ref, buffer, mask = refs[count + aliased :]
     spot = scalars[SPOT]
     total_rows = rows * parts
     speed = speed_ref[scalars[OWN_FIRST] + start + pl.program_id(0)]
-    lane = lax.broadcasted_iota(jnp.int32, (total_rows, LANES), 1)
-    row_zero = jnp.zeros((EDGE, LANES), jnp.float32)
+    step = sub_rows(rows // max(len(pieces) for pieces in layout))
+    lane = lax.broadcasted_iota(jnp.int32, (step, LANES), 1)
     slots = buffer.shape[0]
-    for slot in range(slots):
-        for tile in range(tiles):
-            buffer[slot, tile, :EDGE] = row_zero
-            buffer[slot, tile, EDGE + total_rows :] = row_zero
-
-    def column(tile, j):
+
+    @pl.when((pl.program_id(0) == 0) & (pl.program_id(1) == 0))
+    def _():
+        mask[...] = mask_ref[...].astype(jnp.float32)
+        edge = jnp.zeros((EDGE, LANES), jnp.float32)
+        for slot in range(slots):
+            for tile in range(tiles):
+                buffer[slot, tile, :EDGE] = edge
+                buffer[slot, tile, EDGE + total_rows :] = edge
+
+    def cell(tile, block, low, j):
         at = sum(len(pieces) for pieces in layout[:tile]) * parts
-        pieces = []
-        for index in range(len(layout[tile])):
-            blocks = [ins[at + index * parts + turn][0, j] for turn in range(parts)]
-            pieces.append([pick(blocks, lax.rem(b + parts - spot, parts)) for b in range(parts)])
-        return jnp.concatenate([piece[b] for b in range(parts) for piece in pieces], axis=0)
-
-    def one(j, forward, northward, slot):
-        cells = [column(tile, j) for tile in range(tiles + 2)]
-        weights = face_weights((speed * cos_ref[j]) * geo_ref[0], forward)
-        moved = [pltpu.roll(cell, 1, axis=1) for cell in cells]
-        steps = [cells[0] - moved[0]]
-        for tile in range(1, tiles + 2):
-            steps.append(cells[tile] - jnp.where(lane < 1, moved[tile - 1], moved[tile]))
-
-        def ahead(amount):
-            turned = [None] + [pltpu.roll(step, LANES - amount, axis=1) for step in steps[1:]]
-            return [None] + [
-                jnp.where(lane >= LANES - amount, turned[tile + 1], turned[tile])
-                for tile in range(1, tiles + 1)
-            ]
-
-        if forward:
-            turned = [pltpu.roll(step, 1, axis=1) for step in steps[:-1]]
-            rear = [None] + [
-                jnp.where(lane < 1, turned[tile - 1], turned[tile]) for tile in range(1, tiles + 1)
-            ]
-            spread = (rear, steps, ahead(1))
-        else:
-            spread = (steps, ahead(1), ahead(2))
-        low, mid, high = face_weights(speed * sin_ref[j], northward)
-        for tile in range(tiles):
-            here = slice(tile * LANES, (tile + 1) * LANES)
-            mask = mask_ref[:, here].astype(jnp.float32)
-            swept = cells[tile + 1]
-            for weight, value in zip(weights, spread):
-                swept = swept - weight * value[tile + 1]
-            swept = swept * mask
-            buffer[slot, tile, EDGE : EDGE + total_rows] = swept
-
-            def shifted(amount, tile=tile):
-                return buffer[slot, tile, EDGE + amount : EDGE + amount + total_rows]
-
-            under, over = shifted(-1), shifted(1)
+        length = rows // len(layout[tile])
+        piece, inside = divmod(low, length)
+        held = ins[at + piece * parts : at + (piece + 1) * parts]
+        if step % 8 == 0:
+            return held[block][0, j, inside : inside + step]
+        turn = lax.rem(block + parts - spot, parts)
+        return pick([ref[0, j, inside : inside + step] for ref in held], turn)
+
+    def along_longitude(j, base, forward, slot):
+        for block in range(parts):
+            for low in range(0, rows, step):
+                if step % 8 == 0:
+                    place = pl.multiple_of(lax.rem(spot + block, parts) * rows + low, 8)
+                else:
+                    place = block * rows + low
+                cells = [cell(tile, block, low, j) for tile in range(tiles + 2)]
+                courant = (speed * cos_ref[base + j]) * geo_ref[INVERSE, pl.ds(place, step)]
+                weights = cell_weights(courant)(forward)
+
+                def shifted(amount):
+                    if amount == 0:
+                        return cells[1:-1]
+                    used = cells[:-1] if amount < 0 else [None] + cells[1:]
+                    turned = [
+                        value if value is None else pltpu.roll(value, -amount % LANES, axis=1)
+                        for value in used
+                    ]
+                    if amount < 0:
+                        return [
+                            jnp.where(lane < -amount, turned[tile - 1], turned[tile])
+                            for tile in range(1, tiles + 1)
+                        ]
+                    return [
+                        jnp.where(lane >= LANES - amount, turned[tile + 1], turned[tile])
+                        for tile in range(1, tiles + 1)
+                    ]
+
+                spread = [shifted(amount) for amount in ((-2, -1, 0, 1) if forward else (-1, 0, 1, 2))]
+                for tile in range(tiles):
+                    swept = sum(weight * value[tile] for weight, value in zip(weights, spread))
+                    swept = swept * mask[pl.ds(place, step), tile * LANES : (tile + 1) * LANES]
+                    buffer[slot, tile, pl.ds(EDGE + place, step)] = swept
+
+    def along_latitude(j, base, northward, slot):
+        low, mid, high = face_weights(speed * sin_ref[base + j], northward)
+        block = sub_rows(total_rows)
+        for row in range(0, total_rows, block):
+            here = slice(row, row + block)
             if northward:
-                front = low * under + mid * swept + high * over
-                rear_flux = low * shifted(-2) + mid * under + high * swept
+                weights = (
+                    low * geo_ref[BEHIND_NOT_FIRST_TWO, here],
+                    mid * geo_ref[BEHIND_NOT_FIRST, here] - low * geo_ref[AHEAD_NOT_FIRST, here],
+                    1.0 - mid * geo_ref[AHEAD, here] + high * geo_ref[BEHIND, here],
+                    -high * geo_ref[AHEAD_NOT_LAST, here],
+                )
             else:
-                front = low * swept + mid * over + high * shifted(2)
-                rear_flux = low * under + mid * swept + high * over
-            out_ref[0, j, :, here] = (swept - geo_ref[1] * front + geo_ref[2] * rear_flux) * mask
-
-    angles = [2.0 * math.pi * j / dirs for j in range(dirs)]
-    kinds = [(round(math.cos(angle), 12) >= 0.0, round(math.sin(angle), 12) >= 0.0) for angle in angles]
-    begin = 0
-    while begin < dirs:
-        end = begin
-        while end < dirs and kinds[end] == kinds[begin]:
-            end += 1
-        kind = kinds[begin]
-        whole = (end - begin) // slots
-
-        def body(index, carry, kind=kind, begin=begin):
-            for slot in range(slots):
-                one(begin + index * slots + slot, *kind, slot)
-            return carry
-
-        lax.fori_loop(0, whole, body, 0)
-        for j in range(begin + whole * slots, end):
-            one(j, *kind, 0)
-        begin = end
+                weights = (
+                    low * geo_ref[BEHIND_NOT_FIRST, here],
+                    1.0 - low * geo_ref[AHEAD, here] + mid * geo_ref[BEHIND, here],
+                    high * geo_ref[BEHIND_NOT_LAST, here] - mid * geo_ref[AHEAD_NOT_LAST, here],
+                    -high * geo_ref[AHEAD_NOT_LAST_TWO, here],
+                )
+            for tile in range(tiles):
+                total = 0.0
+                for amount, weight in zip((-2, -1, 0, 1) if northward else (-1, 0, 1, 2), weights):
+                    at = EDGE + row + amount
+                    total = total + weight * buffer[slot, tile, at : at + block]
+                across = slice(tile * LANES, (tile + 1) * LANES)
+                out_ref[0, j, here, across] = total * mask[here, across]
+
+    def quarter(forward, northward):
+        base = pl.program_id(1) * dirs
+
+        for j in range(dirs + 1):
+            if j < dirs:
+                along_longitude(j, base, forward, j % slots)
+            if j > 0:
+                along_latitude(j - 1, base, northward, (j - 1) % slots)
+
+    for index, kind in enumerate(((True, True), (False, True), (False, False), (True, False))):
+        pl.when(pl.program_id(1) == index)(functools.partial(quarter, *kind))
 
 
 def sweep(scalars, speed, cosines, sines, geometry, sea_mask, layout, start, length, freqs, result):
@@ -434,9 +468,12 @@
     flat = [entry for pieces in layout for piece in pieces for entry in piece]
     smem = pl.BlockSpec(memory_space=pltpu.SMEM)
 
+    quarter = dirs // 4
+
     def block(array, origin):
         offset = start - origin
-        return pl.BlockSpec((1,) + array.shape[1:], lambda f: (f + offset, 0, 0, 0))
+        shape = (1, quarter) + array.shape[2:]
+        return pl.BlockSpec(shape, lambda f, q: (f + offset, q, 0, 0))
 
     operands = [array for array, _ in flat]
     specs = [block(array, origin) for array, origin in flat]
@@ -447,20 +484,21 @@
         specs.append(pl.BlockSpec(memory_space=pl.ANY))
     return pl.pallas_call(
         functools.partial(
-            sweep_kernel, parts, [[None] * len(pieces) for pieces in layout], dirs, rows, start,
+            sweep_kernel, parts, [[None] * len(pieces) for pieces in layout], quarter, rows, start,
             len(aliases),
         ),
         out_shape=jax.ShapeDtypeStruct((freqs, dirs, total_rows, width), jnp.float32),
-        grid=(length,),
+        grid=(length, 4),
         in_specs=[smem] * 4
         + [
-            pl.BlockSpec((3, total_rows, LANES), lambda f: (0, 0, 0)),
-            pl.BlockSpec((total_rows, width), lambda f: (0, 0)),
+            pl.BlockSpec(geometry.shape, lambda f, q: (0, 0, 0)),
+            pl.BlockSpec((total_rows, width), lambda f, q: (0, 0)),
         ]
         + specs,
-        out_specs=pl.BlockSpec((1, dirs, total_rows, width), lambda f: (f + start, 0, 0, 0)),
+        out_specs=pl.BlockSpec((1, quarter, total_rows, width), lambda f, q: (f + start, q, 0, 0)),
         scratch_shapes=[
-            pltpu.VMEM((2, width // LANES, total_rows + 2 * EDGE, LANES), jnp.float32)
+            pltpu.VMEM((3, width // LANES, total_rows + 2 * EDGE, LANES), jnp.float32),
+            pltpu.VMEM((total_rows, width), jnp.float32),
         ],
         input_output_aliases=aliases,
         compiler_params=pltpu.CompilerParams(vmem_limit_bytes=VMEM_LIMIT),
@@ -541,7 +579,22 @@
     faces = np.cos(
         np.radians(BAND_CENTRE + (np.arange(band_rows + 1) - band_rows / 2.0) * CELL_DEGREES)
     )
-    geometry = np.stack([1.0 / cells, faces[1:] / cells, faces[:-1] / cells])
+    ahead, behind = faces[1:] / cells, faces[:-1] / cells
+    place = np.arange(band_rows)
+    not_first, not_last = place > 0, place < band_rows - 1
+    geometry = np.stack(
+        [
+            1.0 / cells,
+            ahead,
+            behind,
+            ahead * not_first,
+            behind * not_first,
+            behind * (place > 1),
+            ahead * not_last,
+            behind * not_last,
+            ahead * (place < band_rows - 2),
+        ]
+    )
     geometry = jnp.asarray(np.repeat(geometry[:, :, None], LANES, axis=2), jnp.float32)
 
     along = u_wind * jnp.cos(wind_dir)

time: 310 us -> 303 us (0.977)
  Pallas kernels: 114 us -> 105 us
    pallas_call x2, Pallas kernels: 29.1 us -> 21.2 us  [sweep(): pl.pallas_call(functools.partial(sweep_kernel, parts, [[None] * len(piece...]
where the time goes in v1:
time: 303 us; the launch traced here: 300 us
  waiting for transfers between devices  134 us (44%)
  Pallas kernels  105 us (35%)
  starting transfers between devices  54.1 us (18%)
  local copies, waits for them, and re-layouts  4.1 us (1%)
    ppermute x6, waiting for transfers between devices, shards(): own = [lax.ppermute(value, 'comp', returns[turn]) for value in own]  52.3 us
    pallas_call x5, Pallas kernels, source(): pl.pallas_call(functools.partial(source_kernel, parts, freqs, dirs, rows,...  49.5 us
    ppermute x10, waiting for transfers between devices, shards(): operands.append(lax.ppermute(packed[parts + side], both, pairs))  33.7 us
    ppermute x10, waiting for transfers between devices, shards(): operands.append(lax.ppermute(joined[side], both, pairs))  23.4 us
    pallas_call x2, Pallas kernels, sweep(): pl.pallas_call(functools.partial(sweep_kernel, parts, [[None] * len(piece...  21.2 us
    ppermute x5, waiting for transfers between devices, shards(): lax.ppermute(packed[turn], 'comp', turns[turn])  18.4 us
    pallas_call x5, Pallas kernels, pack(): pl.pallas_call(functools.partial(pack_kernel, parts, rows, low, size, lea...  17.6 us
    pallas_call x5, Pallas kernels, join(): pl.pallas_call(functools.partial(join_kernel, own.shape[0]), out_shape=[s...  17.2 us
  transfers between devices with their start and end apart: 35, of which 13 were waited for; matrix products, arithmetic and copies ran while one was open for 1% of the time, Pallas kernels for 31%

profile of v1, /device:TPU:1, one launch (start us, length us, event | category | flops | bytes accessed | tf_op | source)
XLA Modules:
  0.0 300.1 jit_solution(17667641035736469372)
XLA Ops:
  0.0 0.6 stack.35.scalars
  0.6 3.1 %shard_map.112 = (f32[4,36,8,128]{3,2,1,0:T(8,128)}, f32[4,36,8,128]{3,2,1,0:T(8,128)}, f32[3,36,8,128]{3,2,1,0:T(8,128)}, f32[3,36,8,128]{3,2,1,0:T(8,128)}) custom-call(s32[6]{0:T(128)} %stack.35.scalars, f32[4,36,32,512]{3,2,1,0:T(8,128)} %bitcast.8, s32[32,512]{1,0:T(8,128)} %mask_ref.13), custom_call_target="tpu_custom_call" | custom-call | tf_op jit(solution)/shard_map/pallas_call | solution.py:95
  3.7 2.1 collective-permute-start.27
  5.8 1.0 collective-permute-start.29
  6.8 3.1 %shard_map.109 = (f32[4,36,8,128]{3,2,1,0:T(8,128)}, f32[4,36,8,128]{3,2,1,0:T(8,128)}, f32[3,36,8,128]{3,2,1,0:T(8,128)}, f32[3,36,8,128]{3,2,1,0:T(8,128)}) custom-call(s32[6]{0:T(128)} %stack.35.scalars, f32[4,36,32,512]{3,2,1,0:T(8,128)} %bitcast.9, s32[32,512]{1,0:T(8,128)} %mask_ref.13), custom_call_target="tpu_custom_call" | custom-call | tf_op jit(solution)/shard_map/pallas_call | solution.py:95
  9.9 1.6 collective-permute-start.21
  11.5 1.5 collective-permute-start.23
  13.0 1.2 collective-permute-start.26
  14.3 3.8 %shard_map.106 = (f32[4,36,16,128]{3,2,1,0:T(8,128)}, f32[4,36,16,128]{3,2,1,0:T(8,128)}, f32[3,36,16,128]{3,2,1,0:T(8,128)}, f32[3,36,16,128]{3,2,1,0:T(8,128)}) custom-call(s32[6]{0:T(128)} %stack.35.scalars, f32[4,36,32,512]{3,2,1,0:T(8,128)} %bitcast.10, s32[32,512]{1,0:T(8,128)} %mask_ref.13), custom_call_target="tpu_custom_call" | custom-call | tf_op jit(solution)/shard_map/pallas_call | solution.py:95
  18.2 1.8 collective-permute-start.17
  20.0 5.3 %collective-permute-done.21.refs_2_ = f32[3,36,8,128]{3,2,1,0:T(8,128)S(1)} collective-permute-done((f32[3,36,8,128]{3,2,1,0:T(8,128)}, f32[3,36,8,128]{3,2,1,0:T(8,128)S(1)}, u32[]{:S(2)}, u32[]{:S(2)}) %collective-permute-start.21) | collective-permute-done | bytes 442400 | tf_op jit(solution)/shard_map/ppermute | solution.py:622
  25.4 0.8 copy-done.20
  26.1 1.1 collective-permute-start.20
  27.3 3.8 %shard_map.103 = (f32[4,36,16,128]{3,2,1,0:T(8,128)}, f32[4,36,16,128]{3,2,1,0:T(8,128)}, f32[3,36,16,128]{3,2,1,0:T(8,128)}, f32[3,36,16,128]{3,2,1,0:T(8,128)}) custom-call(s32[6]{0:T(128)} %stack.35.scalars, f32[4,36,32,512]{3,2,1,0:T(8,128)} %bitcast.11, s32[32,512]{1,0:T(8,128)} %mask_ref.13), custom_call_target="tpu_custom_call" | custom-call | tf_op jit(solution)/shard_map/pallas_call | solution.py:95
  31.1 1.4 collective-permute-start.9
  32.7 3.8 %shard_map.100 = (f32[4,36,16,128]{3,2,1,0:T(8,128)}, f32[4,36,16,128]{3,2,1,0:T(8,128)}, f32[3,36,16,128]{3,2,1,0:T(8,128)}, f32[3,36,16,128]{3,2,1,0:T(8,128)}) custom-call(s32[6]{0:T(128)} %stack.35.scalars, f32[4,36,32,512]{3,2,1,0:T(8,128)} %bitcast.12, s32[32,512]{1,0:T(8,128)} %mask_ref.13), custom_call_target="tpu_custom_call" | custom-call | tf_op jit(solution)/shard_map/pallas_call | solution.py:95
  36.5 2.8 collective-permute-done.20.other_ref.refs_1_
  39.2 0.6 collective-permute-start
  39.8 4.6 %collective-permute-done.15.refs_2_ = f32[3,36,16,128]{3,2,1,0:T(8,128)} collective-permute-done((f32[3,36,16,128]{3,2,1,0:T(8,128)}, f32[3,36,16,128]{3,2,1,0:T(8,128)}, u32[]{:S(2)}, u32[]{:S(2)}) %collective-permute-start.15) | collective-permute-done | bytes 884768 | tf_op jit(solution)/shard_map/ppermute | solution.py:622
  44.4 2.2 collective-permute-start.11
  46.9 16.5 %collective-permute-done.9.refs_2_ = f32[3,36,16,128]{3,2,1,0:T(8,128)} collective-permute-done((f32[3,36,16,128]{3,2,1,0:T(8,128)}, f32[3,36,16,128]{3,2,1,0:T(8,128)}, u32[]{:S(2)}, u32[]{:S(2)}) %collective-permute-start.9) | collective-permute-done | bytes 884768 | tf_op jit(solution)/shard_map/ppermute | solution.py:622
  63.4 2.1 collective-permute-start.3
  65.5 3.0 shard_map.113
  68.9 0.6 copy-done.2
  69.5 3.8 %shard_map.104 = (f32[4,36,16,128]{3,2,1,0:T(8,128)}, f32[4,36,16,128]{3,2,1,0:T(8,128)}) custom-call(s32[6]{0:T(128)} %stack.35.scalars, f32[4,36,16,128]{3,2,1,0:T(8,128)} %get-tuple-element.55.own_ref.refs_0_, f32[4,36,16,128]{3,2,1,0:T(8,128)} %copy-done.2), custom_call_target="tpu_custom_call" | custom-call | tf_op jit(solution)/shard_map/pallas_call | solution.py:139
  73.4 1.7 collective-permute-start.14
  75.1 7.3 %collective-permute-done.1.refs_2_ = f32[3,36,16,128]{3,2,1,0:T(8,128)} collective-permute-done((f32[3,36,16,128]{3,2,1,0:T(8,128)}, f32[3,36,16,128]{3,2,1,0:T(8,128)}, u32[]{:S(2)}, u32[]{:S(2)}) %collective-permute-start.1) | collective-permute-done | bytes 884768 | tf_op jit(solution)/shard_map/ppermute | solution.py:622
  82.4 1.2 collective-permute-start.10
  83.5 6.3 %collective-permute-done.other_ref.refs_1_ = f32[4,36,16,128]{3,2,1,0:T(8,128)S(1)} collective-permute-done((f32[4,36,16,128]{3,2,1,0:T(8,128)}, f32[4,36,16,128]{3,2,1,0:T(8,128)S(1)}, u32[]{:S(2)}, u32[]{:S(2)}) %collective-permute-start) | collective-permute-done | bytes 1179680 | tf_op jit(solution)/shard_map/ppermute | solution.py:616
  89.8 5.4 %collective-permute-start.12 = (f32[4,36,16,128]{3,2,1,0:T(8,128)}, f32[4,36,16,128]{3,2,1,0:T(8,128)}, u32[]{:S(2)}, u32[]{:S(2)}) collective-permute-start(f32[4,36,16,128]{3,2,1,0:T(8,128)} %get-tuple-element.60), channel_id=1, source_target_pairs={{0,8},{1,9},{2,4},{3,5},{4,2},{5,3},{6,14},{7,15},{8,0},{9,1},{10,... | collective-permute-start | bytes 3538952 | tf_op jit(solution)/shard_map/ppermute | solution.py:623
  95.2 3.7 %shard_map.101 = (f32[4,36,16,128]{3,2,1,0:T(8,128)}, f32[4,36,16,128]{3,2,1,0:T(8,128)}) custom-call(s32[6]{0:T(128)} %stack.35.scalars, f32[4,36,16,128]{3,2,1,0:T(8,128)} %get-tuple-element.47.own_ref.refs_0_, f32[4,36,16,128]{3,2,1,0:T(8,128)} %copy-done.1), custom_call_target="tpu_custom_call" | custom-call | tf_op jit(solution)/shard_map/pallas_call | solution.py:139
  99.0 3.6 %collective-permute-start.4 = (f32[4,36,16,128]{3,2,1,0:T(8,128)}, f32[4,36,16,128]{3,2,1,0:T(8,128)}, u32[]{:S(2)}, u32[]{:S(2)}) collective-permute-start(f32[4,36,16,128]{3,2,1,0:T(8,128)} %get-tuple-element.52), channel_id=1, source_target_pairs={{0,8},{1,9},{2,4},{3,5},{4,2},{5,3},{6,14},{7,15},{8,0},{9,1},{10,... | collective-permute-start | bytes 3538952 | tf_op jit(solution)/shard_map/ppermute | solution.py:623
  102.6 3.0 %shard_map.110 = (f32[4,36,8,128]{3,2,1,0:T(8,128)}, f32[4,36,8,128]{3,2,1,0:T(8,128)}) custom-call(s32[6]{0:T(128)} %stack.35.scalars, f32[4,36,8,128]{3,2,1,0:T(8,128)} %get-tuple-element.71.own_ref.refs_0_, f32[4,36,8,128]{3,2,1,0:T(8,128)} %copy-done.12), custom_call_target="tpu_custom_call" | custom-call | tf_op jit(solution)/shard_map/pallas_call | solution.py:139
  105.6 9.4 %collective-permute-done.14.other_ref.refs_1_ = f32[4,36,16,128]{3,2,1,0:T(8,128)S(1)} collective-permute-done((f32[4,36,16,128]{3,2,1,0:T(8,128)}, f32[4,36,16,128]{3,2,1,0:T(8,128)S(1)}, u32[]{:S(2)}, u32[]{:S(2)}) %collective-permute-start.14) | collective-permute-done | bytes 1179680 | tf_op jit(solution)/shard_map/ppermute | solution.py:616
  115.0 0.7 collective-permute-start.22
  115.7 4.5 %collective-permute-done.10.refs_3_ = f32[4,36,16,128]{3,2,1,0:T(8,128)S(1)} collective-permute-done((f32[4,36,16,128]{3,2,1,0:T(8,128)}, f32[4,36,16,128]{3,2,1,0:T(8,128)S(1)}, u32[]{:S(2)}, u32[]{:S(2)}) %collective-permute-start.10) | collective-permute-done | bytes 1179680 | tf_op jit(solution)/shard_map/ppermute | solution.py:623
  120.2 2.1 collective-permute-start.24
  122.3 3.7 %shard_map.107 = (f32[4,36,16,128]{3,2,1,0:T(8,128)}, f32[4,36,16,128]{3,2,1,0:T(8,128)}) custom-call(s32[6]{0:T(128)} %stack.35.scalars, f32[4,36,16,128]{3,2,1,0:T(8,128)} %get-tuple-element.63.own_ref.refs_0_, f32[4,36,16,128]{3,2,1,0:T(8,128)} %copy-done), custom_call_target="tpu_custom_call" | custom-call | tf_op jit(solution)/shard_map/pallas_call | solution.py:139
  126.0 0.5 collective-permute-start.16
  126.5 18.9 %collective-permute-done.2.refs_3_ = f32[4,36,16,128]{3,2,1,0:T(8,128)S(1)} collective-permute-done((f32[4,36,16,128]{3,2,1,0:T(8,128)}, f32[4,36,16,128]{3,2,1,0:T(8,128)S(1)}, u32[]{:S(2)}, u32[]{:S(2)}) %collective-permute-start.2) | collective-permute-done | bytes 1179680 | tf_op jit(solution)/shard_map/ppermute | solution.py:623
  145.4 2.1 collective-permute-start.18
  147.6 1.8 sine_multiply_fusion
  149.3 11.6 %shard_map.105 = (f32[4,36,16,128]{3,2,1,0:T(8,128)}, f32[4,36,16,128]{3,2,1,0:T(8,128)}) custom-call(s32[6]{0:T(128)} %stack.35.scalars, f32[32]{0:T(128)} %constant.33.clone.gain_ref, f32[32]{0:T(128)} %constant.34.clone.drop_ref, f32[32,512]{1,0:T(8,128)} %get-tuple-element.90.along_ref, f32[32,512]{1,0:T(8,128)} %get-tuple-element.89.across_ref, ...), custom_call_target="tpu_custom_call" | custom-call | tf_op jit(solution)/shard_map/pallas_call | solution.py:313
  161.2 11.5 %shard_map.102 = (f32[4,36,16,128]{3,2,1,0:T(8,128)}, f32[4,36,16,128]{3,2,1,0:T(8,128)}) custom-call(s32[6]{0:T(128)} %stack.35.scalars, f32[32]{0:T(128)} %constant.33.clone.gain_ref, f32[32]{0:T(128)} %constant.34.clone.drop_ref, f32[32,512]{1,0:T(8,128)} %get-tuple-element.90.along_ref, f32[32,512]{1,0:T(8,128)} %get-tuple-element.89.across_ref, ...), custom_call_target="tpu_custom_call" | custom-call | tf_op jit(solution)/shard_map/pallas_call | solution.py:313
  172.6 1.8 collective-permute-start.13
  174.5 7.5 %shard_map.111 = (f32[4,36,8,128]{3,2,1,0:T(8,128)}, f32[4,36,8,128]{3,2,1,0:T(8,128)}) custom-call(s32[6]{0:T(128)} %stack.35.scalars, f32[32]{0:T(128)} %constant.33.clone.gain_ref, f32[32]{0:T(128)} %constant.34.clone.drop_ref, f32[32,512]{1,0:T(8,128)} %get-tuple-element.90.along_ref, f32[32,512]{1,0:T(8,128)} %get-tuple-element.89.across_ref, ...), custom_call_target="tpu_custom_call" | custom-call | tf_op jit(solution)/shard_map/pallas_call | solution.py:313
  182.0 1.4 collective-permute-start.25
  183.4 7.5 %shard_map.114 = (f32[2,36,8,128]{3,2,1,0:T(8,128)}, f32[2,36,8,128]{3,2,1,0:T(8,128)}, f32[2,36,8,128]{3,2,1,0:T(8,128)}, f32[2,36,8,128]{3,2,1,0:T(8,128)}) custom-call(s32[6]{0:T(128)} %stack.35.scalars, f32[32]{0:T(128)} %constant.33.clone.gain_ref, f32[32]{0:T(128)} %constant.34.clone.drop_ref, f32[32,512]{1,0:T(8,128)} %get-tuple-element.90.along_ref, ...), custom_call_target="tpu_custom_call" | custom-call | tf_op jit(solution)/shard_map/pallas_call | solution.py:313
  191.0 1.0 copy-done.14
  192.0 0.7 collective-permute-start.34
  192.7 11.4 %shard_map.108 = (f32[4,36,16,128]{3,2,1,0:T(8,128)}, f32[4,36,16,128]{3,2,1,0:T(8,128)}) custom-call(s32[6]{0:T(128)} %stack.35.scalars, f32[32]{0:T(128)} %constant.33.clone.gain_ref, f32[32]{0:T(128)} %constant.34.clone.drop_ref, f32[32,512]{1,0:T(8,128)} %get-tuple-element.90.along_ref, f32[32,512]{1,0:T(8,128)} %get-tuple-element.89.across_ref, ...), custom_call_target="tpu_custom_call" | custom-call | tf_op jit(solution)/shard_map/pallas_call | solution.py:313
  204.2 0.8 collective-permute-start.19
  205.0 39.9 %collective-permute-done.34.refs_9_ = f32[2,36,8,128]{3,2,1,0:T(8,128)} collective-permute-done((f32[2,36,8,128]{3,2,1,0:T(8,128)}, f32[2,36,8,128]{3,2,1,0:T(8,128)}, u32[]{:S(2)}, u32[]{:S(2)}) %collective-permute-start.34) | collective-permute-done | bytes 294944 | tf_op jit(solution)/shard_map/ppermute | solution.py:636
  244.9 3.5 %collective-permute-start.32 = (f32[4,36,16,128]{3,2,1,0:T(8,128)S(1)}, f32[4,36,16,128]{3,2,1,0:T(8,128)S(1)}, u32[]{:S(2)}, u32[]{:S(2)}) collective-permute-start(f32[4,36,16,128]{3,2,1,0:T(8,128)S(1)} %copy-done.3), channel_id=1, source_target_pairs={{8,0},{16,8},{24,16},{9,1},{17,9},{25,17},{10,2},{18,10},{26,18},{... | collective-permute-start | bytes 3538952 | tf_op jit(solution)/shard_map/ppermute | solution.py:642
  248.4 3.5 %collective-permute-start.5 = (f32[4,36,16,128]{3,2,1,0:T(8,128)S(1)}, f32[4,36,16,128]{3,2,1,0:T(8,128)S(1)}, u32[]{:S(2)}, u32[]{:S(2)}) collective-permute-start(f32[4,36,16,128]{3,2,1,0:T(8,128)S(1)} %copy-done.4), channel_id=1, source_target_pairs={{0,8},{8,16},{16,24},{1,9},{9,17},{17,25},{2,10},{10,18},{18,26},{... | collective-permute-start | bytes 3538952 | tf_op jit(solution)/shard_map/ppermute | solution.py:642
  251.9 1.9 collective-permute-start.33
  253.8 3.8 %collective-permute-start.7 = (f32[4,36,16,128]{3,2,1,0:T(8,128)}, f32[4,36,16,128]{3,2,1,0:T(8,128)S(1)}, u32[]{:S(2)}, u32[]{:S(2)}) collective-permute-start(f32[4,36,16,128]{3,2,1,0:T(8,128)} %collective-permute-done.6.refs_11_), channel_id=1, source_target_pairs={{0,8},{8,16},{16,24},{1,9},{9,17},{17,25},{2,10},{10,18},{18,26},{... | collective-permute-start | bytes 3538952 | tf_op jit(solution)/shard_map/ppermute | solution.py:642
  257.7 12.4 %collective-permute-done.19.refs_5_ = f32[4,36,16,128]{3,2,1,0:T(8,128)S(1)} collective-permute-done((f32[4,36,16,128]{3,2,1,0:T(8,128)}, f32[4,36,16,128]{3,2,1,0:T(8,128)S(1)}, u32[]{:S(2)}, u32[]{:S(2)}) %collective-permute-start.19) | collective-permute-done | bytes 1179680 | tf_op jit(solution)/shard_map/ppermute | solution.py:636
  270.0 1.2 collective-permute-start.31
  271.3 5.5 %collective-permute-done.33.refs_13_ = f32[4,36,16,128]{3,2,1,0:T(8,128)S(1)} collective-permute-done((f32[4,36,16,128]{3,2,1,0:T(8,128)S(1)}, f32[4,36,16,128]{3,2,1,0:T(8,128)S(1)}, u32[]{:S(2)}, u32[]{:S(2)}) %collective-permute-start.33) | collective-permute-done | bytes 1179680 | tf_op jit(solution)/shard_map/ppermute | solution.py:642
  276.8 0.9 collective-permute-done.7.refs_1_
  277.9 0.9 copy-done.10
  278.8 10.6 %shard_map.115.refs_14_ = f32[4,36,32,512]{3,2,1,0:T(8,128)} custom-call(s32[6]{0:T(128)} %stack.35.scalars, f32[32]{0:T(128)} %constant.35.clone.speed_ref, f32[36]{0:T(128)} %constant.36.clone.cos_ref, f32[36]{0:T(128)} %constant.37.clone.sin_ref, f32[9,32,128]{2,1,0:T(8,128)} %constant.38.clone.geo_ref, s32[32,512]{1,0:T(8,128)} %mask_ref.13, ...), custom_call_target="tpu_custom_call" | custom-call | tf_op jit(solution)/shard_map/pallas_call | solution.py:485
  289.4 10.6 %shard_map.116 = f32[4,36,32,512]{3,2,1,0:T(8,128)} custom-call(s32[6]{0:T(128)} %stack.35.scalars, f32[32]{0:T(128)} %constant.35.clone.speed_ref, f32[36]{0:T(128)} %constant.36.clone.cos_ref, f32[36]{0:T(128)} %constant.37.clone.sin_ref, f32[9,32,128]{2,1,0:T(8,128)} %constant.38.clone.geo_ref, ...), custom_call_target="tpu_custom_call", output_to_operand_aliasing={{}: (20, {})} | custom-call | tf_op jit(solution)/shard_map/pallas_call | solution.py:485
  (73 shorter events, 1.7 us)
Async XLA Ops:
  3.7 14.4 %collective-permute-start.27 = (f32[3,36,8,128]{3,2,1,0:T(8,128)}, f32[3,36,8,128]{3,2,1,0:T(8,128)S(1)}, u32[]{:S(2)}, u32[]{:S(2)}) collective-permute-start(f32[3,36,8,128]{3,2,1,0:T(8,128)} %get-tuple-element.81), channel_id=1, source_target_pairs={{0,2},{1,3},{2,0},{3,1},{4,6},{5,7},{6,4},{7,5},{8,10},{9,11},{10,... | collective-permute-start | bytes 1327112 | tf_op jit(solution)/shard_map/ppermute | solution.py:622
  5.8 7.2 %copy-start.23 = (f32[4,36,8,128]{3,2,1,0:T(8,128)S(1)}, f32[4,36,8,128]{3,2,1,0:T(8,128)}, u32[]{:S(2)}) copy-start(f32[4,36,8,128]{3,2,1,0:T(8,128)} %get-tuple-element.80) | copy-start | bytes 1769476
  5.8 12.4 %collective-permute-start.29 = (f32[3,36,8,128]{3,2,1,0:T(8,128)}, f32[3,36,8,128]{3,2,1,0:T(8,128)S(1)}, u32[]{:S(2)}, u32[]{:S(2)}) collective-permute-start(f32[3,36,8,128]{3,2,1,0:T(8,128)} %get-tuple-element.83), channel_id=1, source_target_pairs={{0,8},{1,9},{2,4},{3,5},{4,2},{5,3},{6,14},{7,15},{8,0},{9,1},{10,... | collective-permute-start | bytes 1327112 | tf_op jit(solution)/shard_map/ppermute | solution.py:622
  9.9 15.5 %collective-permute-start.21 = (f32[3,36,8,128]{3,2,1,0:T(8,128)}, f32[3,36,8,128]{3,2,1,0:T(8,128)S(1)}, u32[]{:S(2)}, u32[]{:S(2)}) collective-permute-start(f32[3,36,8,128]{3,2,1,0:T(8,128)} %get-tuple-element.73), channel_id=1, source_target_pairs={{0,2},{1,3},{2,0},{3,1},{4,6},{5,7},{6,4},{7,5},{8,10},{9,11},{10,... | collective-permute-start | bytes 1327112 | tf_op jit(solution)/shard_map/ppermute | solution.py:622
  11.5 19.6 %collective-permute-start.23 = (f32[3,36,8,128]{3,2,1,0:T(8,128)}, f32[3,36,8,128]{3,2,1,0:T(8,128)S(1)}, u32[]{:S(2)}, u32[]{:S(2)}) collective-permute-start(f32[3,36,8,128]{3,2,1,0:T(8,128)} %get-tuple-element.75), channel_id=1, source_target_pairs={{0,8},{1,9},{2,4},{3,5},{4,2},{5,3},{6,14},{7,15},{8,0},{9,1},{10,... | collective-permute-start | bytes 1327112 | tf_op jit(solution)/shard_map/ppermute | solution.py:622
  13.0 19.4 %collective-permute-start.26 = (f32[4,36,8,128]{3,2,1,0:T(8,128)S(1)}, f32[4,36,8,128]{3,2,1,0:T(8,128)S(1)}, u32[]{:S(2)}, u32[]{:S(2)}) collective-permute-start(f32[4,36,8,128]{3,2,1,0:T(8,128)S(1)} %copy-done.23), channel_id=1, source_target_pairs={{0,1},{1,0},{2,3},{3,2},{4,5},{5,4},{6,7},{7,6},{8,9},{9,8},{10,11... | collective-permute-start | bytes 1769480 | tf_op jit(solution)/shard_map/ppermute | solution.py:616
  18.1 13.0 %copy-start.18 = (f32[3,36,8,128]{3,2,1,0:T(8,128)}, f32[3,36,8,128]{3,2,1,0:T(8,128)S(1)}, u32[]{:S(2)}) copy-start(f32[3,36,8,128]{3,2,1,0:T(8,128)S(1)} %collective-permute-done.27.refs_2_) | copy-start | bytes 1327108
  18.1 26.3 %collective-permute-start.15 = (f32[3,36,16,128]{3,2,1,0:T(8,128)}, f32[3,36,16,128]{3,2,1,0:T(8,128)}, u32[]{:S(2)}, u32[]{:S(2)}) collective-permute-start(f32[3,36,16,128]{3,2,1,0:T(8,128)} %get-tuple-element.65), channel_id=1, source_target_pairs={{0,2},{1,3},{2,0},{3,1},{4,6},{5,7},{6,4},{7,5},{8,10},{9,11},{10,... | collective-permute-start | bytes 2654216 | tf_op jit(solution)/shard_map/ppermute | solution.py:622
  18.2 7.2 %copy-start.19 = (f32[3,36,8,128]{3,2,1,0:T(8,128)}, f32[3,36,8,128]{3,2,1,0:T(8,128)S(1)}, u32[]{:S(2)}) copy-start(f32[3,36,8,128]{3,2,1,0:T(8,128)S(1)} %collective-permute-done.29.refs_4_) | copy-start | bytes 1327108
  18.2 28.4 %collective-permute-start.17 = (f32[3,36,16,128]{3,2,1,0:T(8,128)}, f32[3,36,16,128]{3,2,1,0:T(8,128)}, u32[]{:S(2)}, u32[]{:S(2)}) collective-permute-start(f32[3,36,16,128]{3,2,1,0:T(8,128)} %get-tuple-element.67), channel_id=1, source_target_pairs={{0,8},{1,9},{2,4},{3,5},{4,2},{5,3},{6,14},{7,15},{8,0},{9,1},{10,... | collective-permute-start | bytes 2654216 | tf_op jit(solution)/shard_map/ppermute | solution.py:622
  25.4 0.8 copy-start.20
  26.1 13.1 %collective-permute-start.20 = (f32[4,36,8,128]{3,2,1,0:T(8,128)}, f32[4,36,8,128]{3,2,1,0:T(8,128)S(1)}, u32[]{:S(2)}, u32[]{:S(2)}) collective-permute-start(f32[4,36,8,128]{3,2,1,0:T(8,128)} %get-tuple-element.72), channel_id=1, source_target_pairs={{0,1},{1,0},{2,3},{3,2},{4,5},{5,4},{6,7},{7,6},{8,9},{9,8},{10,11... | collective-permute-start | bytes 1769480 | tf_op jit(solution)/shard_map/ppermute | solution.py:616
  31.1 5.4 %copy-start.21 = (f32[3,36,8,128]{3,2,1,0:T(8,128)}, f32[3,36,8,128]{3,2,1,0:T(8,128)S(1)}, u32[]{:S(2)}) copy-start(f32[3,36,8,128]{3,2,1,0:T(8,128)S(1)} %collective-permute-done.23.refs_4_) | copy-start | bytes 1327108
  31.1 32.3 %collective-permute-start.9 = (f32[3,36,16,128]{3,2,1,0:T(8,128)}, f32[3,36,16,128]{3,2,1,0:T(8,128)}, u32[]{:S(2)}, u32[]{:S(2)}) collective-permute-start(f32[3,36,16,128]{3,2,1,0:T(8,128)} %get-tuple-element.57), channel_id=1, source_target_pairs={{0,2},{1,3},{2,0},{3,1},{4,6},{5,7},{6,4},{7,5},{8,10},{9,11},{10,... | collective-permute-start | bytes 2654216 | tf_op jit(solution)/shard_map/ppermute | solution.py:622
  32.4 4.0 %copy-start.11 = (f32[4,36,8,128]{3,2,1,0:T(8,128)}, f32[4,36,8,128]{3,2,1,0:T(8,128)S(1)}, u32[]{:S(2)}) copy-start(f32[4,36,8,128]{3,2,1,0:T(8,128)S(1)} %collective-permute-done.26.other_ref.refs_1_) | copy-start | bytes 1769476
  32.4 36.1 %collective-permute-start.8 = (f32[4,36,16,128]{3,2,1,0:T(8,128)}, f32[4,36,16,128]{3,2,1,0:T(8,128)S(1)}, u32[]{:S(2)}, u32[]{:S(2)}) collective-permute-start(f32[4,36,16,128]{3,2,1,0:T(8,128)} %get-tuple-element.56), channel_id=1, source_target_pairs={{0,1},{1,0},{2,3},{3,2},{4,5},{5,4},{6,7},{7,6},{8,9},{9,8},{10,11... | collective-permute-start | bytes 3538952 | tf_op jit(solution)/shard_map/ppermute | solution.py:616
  39.2 34.1 %copy-start.12 = (f32[4,36,8,128]{3,2,1,0:T(8,128)}, f32[4,36,8,128]{3,2,1,0:T(8,128)S(1)}, u32[]{:S(2)}) copy-start(f32[4,36,8,128]{3,2,1,0:T(8,128)S(1)} %collective-permute-done.20.other_ref.refs_1_) | copy-start | bytes 1769476
  39.2 50.6 %collective-permute-start = (f32[4,36,16,128]{3,2,1,0:T(8,128)}, f32[4,36,16,128]{3,2,1,0:T(8,128)S(1)}, u32[]{:S(2)}, u32[]{:S(2)}) collective-permute-start(f32[4,36,16,128]{3,2,1,0:T(8,128)} %get-tuple-element.48), channel_id=1, source_target_pairs={{0,1},{1,0},{2,3},{3,2},{4,5},{5,4},{6,7},{7,6},{8,9},{9,8},{10,11... | collective-permute-start | bytes 3538952 | tf_op jit(solution)/shard_map/ppermute | solution.py:616
  44.4 28.9 %collective-permute-start.11 = (f32[3,36,16,128]{3,2,1,0:T(8,128)}, f32[3,36,16,128]{3,2,1,0:T(8,128)}, u32[]{:S(2)}, u32[]{:S(2)}) collective-permute-start(f32[3,36,16,128]{3,2,1,0:T(8,128)} %get-tuple-element.59), channel_id=1, source_target_pairs={{0,8},{1,9},{2,4},{3,5},{4,2},{5,3},{6,14},{7,15},{8,0},{9,1},{10,... | collective-permute-start | bytes 2654216 | tf_op jit(solution)/shard_map/ppermute | solution.py:622
  46.6 35.7 %collective-permute-start.1 = (f32[3,36,16,128]{3,2,1,0:T(8,128)}, f32[3,36,16,128]{3,2,1,0:T(8,128)}, u32[]{:S(2)}, u32[]{:S(2)}) collective-permute-start(f32[3,36,16,128]{3,2,1,0:T(8,128)} %get-tuple-element.49), channel_id=1, source_target_pairs={{0,2},{1,3},{2,0},{3,1},{4,6},{5,7},{6,4},{7,5},{8,10},{9,11},{10,... | collective-permute-start | bytes 2654216 | tf_op jit(solution)/shard_map/ppermute | solution.py:622
  63.4 35.5 %collective-permute-start.3 = (f32[3,36,16,128]{3,2,1,0:T(8,128)}, f32[3,36,16,128]{3,2,1,0:T(8,128)}, u32[]{:S(2)}, u32[]{:S(2)}) collective-permute-start(f32[3,36,16,128]{3,2,1,0:T(8,128)} %get-tuple-element.51), channel_id=1, source_target_pairs={{0,8},{1,9},{2,4},{3,5},{4,2},{5,3},{6,14},{7,15},{8,0},{9,1},{10,... | collective-permute-start | bytes 2654216 | tf_op jit(solution)/shard_map/ppermute | solution.py:622
  68.5 1.1 copy-start.2
  68.5 30.5 %collective-permute-start.28 = (f32[4,36,8,128]{3,2,1,0:T(8,128)}, f32[4,36,8,128]{3,2,1,0:T(8,128)}, u32[]{:S(2)}, u32[]{:S(2)}) collective-permute-start(f32[4,36,8,128]{3,2,1,0:T(8,128)} %get-tuple-element.82), channel_id=1, source_target_pairs={{0,2},{1,3},{2,0},{3,1},{4,6},{5,7},{6,4},{7,5},{8,10},{9,11},{10,... | collective-permute-start | bytes 1769480 | tf_op jit(solution)/shard_map/ppermute | solution.py:623
  73.4 41.6 %collective-permute-start.14 = (f32[4,36,16,128]{3,2,1,0:T(8,128)}, f32[4,36,16,128]{3,2,1,0:T(8,128)S(1)}, u32[]{:S(2)}, u32[]{:S(2)}) collective-permute-start(f32[4,36,16,128]{3,2,1,0:T(8,128)} %get-tuple-element.64), channel_id=1, source_target_pairs={{0,1},{1,0},{2,3},{3,2},{4,5},{5,4},{6,7},{7,6},{8,9},{9,8},{10,11... | collective-permute-start | bytes 3538952 | tf_op jit(solution)/shard_map/ppermute | solution.py:616
  82.4 37.8 %collective-permute-start.10 = (f32[4,36,16,128]{3,2,1,0:T(8,128)}, f32[4,36,16,128]{3,2,1,0:T(8,128)S(1)}, u32[]{:S(2)}, u32[]{:S(2)}) collective-permute-start(f32[4,36,16,128]{3,2,1,0:T(8,128)} %get-tuple-element.58), channel_id=1, source_target_pairs={{0,2},{1,3},{2,0},{3,1},{4,6},{5,7},{6,4},{7,5},{8,10},{9,11},{10,... | collective-permute-start | bytes 3538952 | tf_op jit(solution)/shard_map/ppermute | solution.py:623
  89.8 5.4 %copy-start.1 = (f32[4,36,16,128]{3,2,1,0:T(8,128)}, f32[4,36,16,128]{3,2,1,0:T(8,128)S(1)}, u32[]{:S(2)}) copy-start(f32[4,36,16,128]{3,2,1,0:T(8,128)S(1)} %collective-permute-done.other_ref.refs_1_) | copy-start | bytes 3538948
  89.8 36.2 %collective-permute-start.12 = (f32[4,36,16,128]{3,2,1,0:T(8,128)}, f32[4,36,16,128]{3,2,1,0:T(8,128)}, u32[]{:S(2)}, u32[]{:S(2)}) collective-permute-start(f32[4,36,16,128]{3,2,1,0:T(8,128)} %get-tuple-element.60), channel_id=1, source_target_pairs={{0,8},{1,9},{2,4},{3,5},{4,2},{5,3},{6,14},{7,15},{8,0},{9,1},{10,... | collective-permute-start | bytes 3538952 | tf_op jit(solution)/shard_map/ppermute | solution.py:623
  98.9 46.5 %collective-permute-start.2 = (f32[4,36,16,128]{3,2,1,0:T(8,128)}, f32[4,36,16,128]{3,2,1,0:T(8,128)S(1)}, u32[]{:S(2)}, u32[]{:S(2)}) collective-permute-start(f32[4,36,16,128]{3,2,1,0:T(8,128)} %get-tuple-element.50), channel_id=1, source_target_pairs={{0,2},{1,3},{2,0},{3,1},{4,6},{5,7},{6,4},{7,5},{8,10},{9,11},{10,... | collective-permute-start | bytes 3538952 | tf_op jit(solution)/shard_map/ppermute | solution.py:623
  99.0 61.9 %collective-permute-start.4 = (f32[4,36,16,128]{3,2,1,0:T(8,128)}, f32[4,36,16,128]{3,2,1,0:T(8,128)}, u32[]{:S(2)}, u32[]{:S(2)}) collective-permute-start(f32[4,36,16,128]{3,2,1,0:T(8,128)} %get-tuple-element.52), channel_id=1, source_target_pairs={{0,8},{1,9},{2,4},{3,5},{4,2},{5,3},{6,14},{7,15},{8,0},{9,1},{10,... | collective-permute-start | bytes 3538952 | tf_op jit(solution)/shard_map/ppermute | solution.py:623
  115.0 7.3 %copy-start = (f32[4,36,16,128]{3,2,1,0:T(8,128)}, f32[4,36,16,128]{3,2,1,0:T(8,128)S(1)}, u32[]{:S(2)}) copy-start(f32[4,36,16,128]{3,2,1,0:T(8,128)S(1)} %collective-permute-done.14.other_ref.refs_1_) | copy-start | bytes 3538948
  115.0 57.6 %collective-permute-start.22 = (f32[4,36,8,128]{3,2,1,0:T(8,128)}, f32[4,36,8,128]{3,2,1,0:T(8,128)}, u32[]{:S(2)}, u32[]{:S(2)}) collective-permute-start(f32[4,36,8,128]{3,2,1,0:T(8,128)} %get-tuple-element.74), channel_id=1, source_target_pairs={{0,2},{1,3},{2,0},{3,1},{4,6},{5,7},{6,4},{7,5},{8,10},{9,11},{10,... | collective-permute-start | bytes 1769480 | tf_op jit(solution)/shard_map/ppermute | solution.py:623
  120.2 5.8 %copy-start.15 = (f32[4,36,16,128]{3,2,1,0:T(8,128)}, f32[4,36,16,128]{3,2,1,0:T(8,128)S(1)}, u32[]{:S(2)}) copy-start(f32[4,36,16,128]{3,2,1,0:T(8,128)S(1)} %collective-permute-done.10.refs_3_) | copy-start | bytes 3538948
  120.2 54.2 %collective-permute-start.24 = (f32[4,36,8,128]{3,2,1,0:T(8,128)}, f32[4,36,8,128]{3,2,1,0:T(8,128)}, u32[]{:S(2)}, u32[]{:S(2)}) collective-permute-start(f32[4,36,8,128]{3,2,1,0:T(8,128)} %get-tuple-element.76), channel_id=1, source_target_pairs={{0,8},{1,9},{2,4},{3,5},{4,2},{5,3},{6,14},{7,15},{8,0},{9,1},{10,... | collective-permute-start | bytes 1769480 | tf_op jit(solution)/shard_map/ppermute | solution.py:623
  126.0 65.0 %collective-permute-start.16 = (f32[4,36,16,128]{3,2,1,0:T(8,128)}, f32[4,36,16,128]{3,2,1,0:T(8,128)S(1)}, u32[]{:S(2)}, u32[]{:S(2)}) collective-permute-start(f32[4,36,16,128]{3,2,1,0:T(8,128)} %get-tuple-element.66), channel_id=1, source_target_pairs={{0,2},{1,3},{2,0},{3,1},{4,6},{5,7},{6,4},{7,5},{8,10},{9,11},{10,... | collective-permute-start | bytes 3538952 | tf_op jit(solution)/shard_map/ppermute | solution.py:623
  145.4 15.5 %copy-start.16 = (f32[4,36,16,128]{3,2,1,0:T(8,128)}, f32[4,36,16,128]{3,2,1,0:T(8,128)S(1)}, u32[]{:S(2)}) copy-start(f32[4,36,16,128]{3,2,1,0:T(8,128)S(1)} %collective-permute-done.2.refs_3_) | copy-start | bytes 3538948
  145.4 47.3 %collective-permute-start.18 = (f32[4,36,16,128]{3,2,1,0:T(8,128)}, f32[4,36,16,128]{3,2,1,0:T(8,128)}, u32[]{:S(2)}, u32[]{:S(2)}) collective-permute-start(f32[4,36,16,128]{3,2,1,0:T(8,128)} %get-tuple-element.68), channel_id=1, source_target_pairs={{0,8},{1,9},{2,4},{3,5},{4,2},{5,3},{6,14},{7,15},{8,0},{9,1},{10,... | collective-permute-start | bytes 3538952 | tf_op jit(solution)/shard_map/ppermute | solution.py:623
  149.3 11.6 %copy-start.22 = (f32[4,36,8,128]{3,2,1,0:T(8,128)S(1)}, f32[4,36,8,128]{3,2,1,0:T(8,128)}, u32[]{:S(2)}) copy-start(f32[4,36,8,128]{3,2,1,0:T(8,128)} %get-tuple-element.84) | copy-start | bytes 1769476
  160.9 21.0 %collective-permute-start.30 = (f32[4,36,8,128]{3,2,1,0:T(8,128)S(1)}, f32[4,36,8,128]{3,2,1,0:T(8,128)S(1)}, u32[]{:S(2)}, u32[]{:S(2)}) collective-permute-start(f32[4,36,8,128]{3,2,1,0:T(8,128)S(1)} %copy-done.22), channel_id=1, source_target_pairs={{0,8},{1,9},{2,4},{3,5},{4,2},{5,3},{6,14},{7,15},{8,0},{9,1},{10,... | collective-permute-start | bytes 1769480 | tf_op jit(solution)/shard_map/ppermute | solution.py:623
  172.6 79.2 %collective-permute-start.13 = (f32[4,36,16,128]{3,2,1,0:T(8,128)}, f32[4,36,16,128]{3,2,1,0:T(8,128)S(1)}, u32[]{:S(2)}, u32[]{:S(2)}) collective-permute-start(f32[4,36,16,128]{3,2,1,0:T(8,128)} %get-tuple-element.62), channel_id=1, source_target_pairs={{1,0},{0,1},{3,2},{2,3},{5,4},{4,5},{7,6},{6,7},{9,8},{8,9},{11,10... | collective-permute-start | bytes 3538952 | tf_op jit(solution)/shard_map/ppermute | solution.py:636
  174.4 79.4 %collective-permute-start.6 = (f32[4,36,16,128]{3,2,1,0:T(8,128)}, f32[4,36,16,128]{3,2,1,0:T(8,128)}, u32[]{:S(2)}, u32[]{:S(2)}) collective-permute-start(f32[4,36,16,128]{3,2,1,0:T(8,128)} %get-tuple-element.54), channel_id=1, source_target_pairs={{1,0},{0,1},{3,2},{2,3},{5,4},{4,5},{7,6},{6,7},{9,8},{8,9},{11,10... | collective-permute-start | bytes 3538952 | tf_op jit(solution)/shard_map/ppermute | solution.py:636
  182.0 1.5 copy-start.17
  182.0 66.4 %collective-permute-start.25 = (f32[4,36,8,128]{3,2,1,0:T(8,128)}, f32[4,36,8,128]{3,2,1,0:T(8,128)S(1)}, u32[]{:S(2)}, u32[]{:S(2)}) collective-permute-start(f32[4,36,8,128]{3,2,1,0:T(8,128)} %get-tuple-element.78), channel_id=1, source_target_pairs={{1,0},{0,1},{3,2},{2,3},{5,4},{4,5},{7,6},{6,7},{9,8},{8,9},{11,10... | collective-permute-start | bytes 1769480 | tf_op jit(solution)/shard_map/ppermute | solution.py:636
  191.0 1.0 copy-start.14
  192.0 52.9 %copy-start.3 = (f32[4,36,16,128]{3,2,1,0:T(8,128)S(1)}, f32[4,36,16,128]{3,2,1,0:T(8,128)}, u32[]{:S(2)}) copy-start(f32[4,36,16,128]{3,2,1,0:T(8,128)} %get-tuple-element.61.refs_2_) | copy-start | bytes 3538948
  192.0 56.4 %copy-start.4 = (f32[4,36,16,128]{3,2,1,0:T(8,128)S(1)}, f32[4,36,16,128]{3,2,1,0:T(8,128)}, u32[]{:S(2)}) copy-start(f32[4,36,16,128]{3,2,1,0:T(8,128)} %get-tuple-element.53.refs_10_) | copy-start | bytes 3538948
  192.0 52.9 %collective-permute-start.34 = (f32[2,36,8,128]{3,2,1,0:T(8,128)}, f32[2,36,8,128]{3,2,1,0:T(8,128)}, u32[]{:S(2)}, u32[]{:S(2)}) collective-permute-start(f32[2,36,8,128]{3,2,1,0:T(8,128)} %get-tuple-element.88), channel_id=1, source_target_pairs={{1,0},{0,1},{3,2},{2,3},{5,4},{4,5},{7,6},{6,7},{9,8},{8,9},{11,10... | collective-permute-start | bytes 884744 | tf_op jit(solution)/shard_map/ppermute | solution.py:636
  204.2 65.9 %collective-permute-start.19 = (f32[4,36,16,128]{3,2,1,0:T(8,128)}, f32[4,36,16,128]{3,2,1,0:T(8,128)S(1)}, u32[]{:S(2)}, u32[]{:S(2)}) collective-permute-start(f32[4,36,16,128]{3,2,1,0:T(8,128)} %get-tuple-element.70), channel_id=1, source_target_pairs={{1,0},{0,1},{3,2},{2,3},{5,4},{4,5},{7,6},{6,7},{9,8},{8,9},{11,10... | collective-permute-start | bytes 3538952 | tf_op jit(solution)/shard_map/ppermute | solution.py:636
  244.9 26.4 %collective-permute-start.32 = (f32[4,36,16,128]{3,2,1,0:T(8,128)S(1)}, f32[4,36,16,128]{3,2,1,0:T(8,128)S(1)}, u32[]{:S(2)}, u32[]{:S(2)}) collective-permute-start(f32[4,36,16,128]{3,2,1,0:T(8,128)S(1)} %copy-done.3), channel_id=1, source_target_pairs={{8,0},{16,8},{24,16},{9,1},{17,9},{25,17},{10,2},{18,10},{26,18},{... | collective-permute-start | bytes 3538952 | tf_op jit(solution)/shard_map/ppermute | solution.py:642
  248.4 30.4 %copy-start.13 = (f32[4,36,8,128]{3,2,1,0:T(8,128)}, f32[4,36,8,128]{3,2,1,0:T(8,128)S(1)}, u32[]{:S(2)}) copy-start(f32[4,36,8,128]{3,2,1,0:T(8,128)S(1)} %collective-permute-done.25.refs_7_) | copy-start | bytes 1769476
  248.4 22.9 %collective-permute-start.5 = (f32[4,36,16,128]{3,2,1,0:T(8,128)S(1)}, f32[4,36,16,128]{3,2,1,0:T(8,128)S(1)}, u32[]{:S(2)}, u32[]{:S(2)}) collective-permute-start(f32[4,36,16,128]{3,2,1,0:T(8,128)S(1)} %copy-done.4), channel_id=1, source_target_pairs={{0,8},{8,16},{16,24},{1,9},{9,17},{17,25},{2,10},{10,18},{18,26},{... | collective-permute-start | bytes 3538952 | tf_op jit(solution)/shard_map/ppermute | solution.py:642
  251.9 26.9 %copy-start.5 = (f32[4,36,16,128]{3,2,1,0:T(8,128)}, f32[4,36,16,128]{3,2,1,0:T(8,128)S(1)}, u32[]{:S(2)}) copy-start(f32[4,36,16,128]{3,2,1,0:T(8,128)S(1)} %collective-permute-done.13.refs_3_) | copy-start | bytes 3538948
  251.9 24.9 %collective-permute-start.33 = (f32[4,36,16,128]{3,2,1,0:T(8,128)S(1)}, f32[4,36,16,128]{3,2,1,0:T(8,128)S(1)}, u32[]{:S(2)}, u32[]{:S(2)}) collective-permute-start(f32[4,36,16,128]{3,2,1,0:T(8,128)S(1)} %collective-permute-done.13.refs_3_), channel_id=1, source_target_pairs={{8,0},{16,8},{24,16},{9,1},{17,9},{25,17},{10,2},{18,10},{26,18},{... | collective-permute-start | bytes 3538952 | tf_op jit(solution)/shard_map/ppermute | solution.py:642
  253.8 23.9 %collective-permute-start.7 = (f32[4,36,16,128]{3,2,1,0:T(8,128)}, f32[4,36,16,128]{3,2,1,0:T(8,128)S(1)}, u32[]{:S(2)}, u32[]{:S(2)}) collective-permute-start(f32[4,36,16,128]{3,2,1,0:T(8,128)} %collective-permute-done.6.refs_11_), channel_id=1, source_target_pairs={{0,8},{8,16},{16,24},{1,9},{9,17},{17,25},{2,10},{10,18},{18,26},{... | collective-permute-start | bytes 3538952 | tf_op jit(solution)/shard_map/ppermute | solution.py:642
  270.0 6.8 %copy-start.6 = (f32[4,36,16,128]{3,2,1,0:T(8,128)}, f32[4,36,16,128]{3,2,1,0:T(8,128)S(1)}, u32[]{:S(2)}) copy-start(f32[4,36,16,128]{3,2,1,0:T(8,128)S(1)} %collective-permute-done.19.refs_5_) | copy-start | bytes 3538948
  270.0 19.3 %collective-permute-start.31 = (f32[2,36,8,128]{3,2,1,0:T(8,128)}, f32[2,36,8,128]{3,2,1,0:T(8,128)}, u32[]{:S(2)}, u32[]{:S(2)}) collective-permute-start(f32[2,36,8,128]{3,2,1,0:T(8,128)} %get-tuple-element.86), channel_id=1, source_target_pairs={{1,0},{0,1},{3,2},{2,3},{5,4},{4,5},{7,6},{6,7},{9,8},{8,9},{11,10... | collective-permute-start | bytes 884744 | tf_op jit(solution)/shard_map/ppermute | solution.py:636
  271.3 6.5 %copy-start.7 = (f32[4,36,16,128]{3,2,1,0:T(8,128)}, f32[4,36,16,128]{3,2,1,0:T(8,128)S(1)}, u32[]{:S(2)}) copy-start(f32[4,36,16,128]{3,2,1,0:T(8,128)S(1)} %collective-permute-done.32.refs_12_) | copy-start | bytes 3538948
  271.3 6.5 %copy-start.8 = (f32[4,36,16,128]{3,2,1,0:T(8,128)}, f32[4,36,16,128]{3,2,1,0:T(8,128)S(1)}, u32[]{:S(2)}) copy-start(f32[4,36,16,128]{3,2,1,0:T(8,128)S(1)} %collective-permute-done.5.refs_0_) | copy-start | bytes 3538948
  276.8 1.1 copy-start.9
  277.7 1.0 copy-start.10

commit v2 on v1

--- a/solution.py
+++ b/solution.py
@@ -447,17 +447,26 @@
                 across = slice(tile * LANES, (tile + 1) * LANES)
                 out_ref[0, j, here, across] = total * mask[here, across]
 
-    def quarter(forward, northward):
-        base = pl.program_id(1) * dirs
-
-        for j in range(dirs + 1):
-            if j < dirs:
+    base = pl.program_id(1) * dirs
+    share = dirs // 2
+
+    def quarter(begin, forward, northward):
+        for j in range(begin, begin + share + 1):
+            if j < begin + share:
                 along_longitude(j, base, forward, j % slots)
-            if j > 0:
+            if j > begin:
                 along_latitude(j - 1, base, northward, (j - 1) % slots)
 
-    for index, kind in enumerate(((True, True), (False, True), (False, False), (True, False))):
-        pl.when(pl.program_id(1) == index)(functools.partial(quarter, *kind))
+    def northern():
+        quarter(0, True, True)
+        quarter(share, False, True)
+
+    def southern():
+        quarter(0, False, False)
+        quarter(share, True, False)
+
+    pl.when(pl.program_id(1) == 0)(northern)
+    pl.when(pl.program_id(1) == 1)(southern)
 
 
 def sweep(scalars, speed, cosines, sines, geometry, sea_mask, layout, start, length, freqs, result):
@@ -468,11 +477,11 @@
     flat = [entry for pieces in layout for piece in pieces for entry in piece]
     smem = pl.BlockSpec(memory_space=pltpu.SMEM)
 
-    quarter = dirs // 4
+    half_circle = dirs // 2
 
     def block(array, origin):
         offset = start - origin
-        shape = (1, quarter) + array.shape[2:]
+        shape = (1, half_circle) + array.shape[2:]
         return pl.BlockSpec(shape, lambda f, q: (f + offset, q, 0, 0))
 
     operands = [array for array, _ in flat]
@@ -484,18 +493,18 @@
         specs.append(pl.BlockSpec(memory_space=pl.ANY))
     return pl.pallas_call(
         functools.partial(
-            sweep_kernel, parts, [[None] * len(pieces) for pieces in layout], quarter, rows, start,
+            sweep_kernel, parts, [[None] * len(pieces) for pieces in layout], half_circle, rows, start,
             len(aliases),
         ),
         out_shape=jax.ShapeDtypeStruct((freqs, dirs, total_rows, width), jnp.float32),
-        grid=(length, 4),
+        grid=(length, 2),
         in_specs=[smem] * 4
         + [
             pl.BlockSpec(geometry.shape, lambda f, q: (0, 0, 0)),
             pl.BlockSpec((total_rows, width), lambda f, q: (0, 0)),
         ]
         + specs,
-        out_specs=pl.BlockSpec((1, quarter, total_rows, width), lambda f, q: (f + start, q, 0, 0)),
+        out_specs=pl.BlockSpec((1, half_circle, total_rows, width), lambda f, q: (f + start, q, 0, 0)),
         scratch_shapes=[
             pltpu.VMEM((3, width // LANES, total_rows + 2 * EDGE, LANES), jnp.float32),
             pltpu.VMEM((total_rows, width), jnp.float32),

time: 303 us -> 299 us (0.987)
    pallas_call x2, Pallas kernels: 21.2 us -> 17.7 us  [sweep(): pl.pallas_call(functools.partial(sweep_kernel, parts, [[None] * len(piece...]
  transfers between devices with their start and end apart: 35 -> 35, of which waited for: 13 -> 13; matrix products, arithmetic and copies ran while one was open for 1% -> 1% of each run, Pallas kernels for 31% -> 30%
where the time goes in v2:
time: 299 us; the launch traced here: 297 us
  waiting for transfers between devices  134 us (45%)
  Pallas kernels  102 us (34%)
  starting transfers between devices  54.1 us (18%)
  local copies, waits for them, and re-layouts  4.1 us (1%)
    ppermute x6, waiting for transfers between devices, shards(): own = [lax.ppermute(value, 'comp', returns[turn]) for value in own]  52.3 us
    pallas_call x5, Pallas kernels, source(): pl.pallas_call(functools.partial(source_kernel, parts, freqs, dirs, rows,...  49.5 us
    ppermute x10, waiting for transfers between devices, shards(): operands.append(lax.ppermute(packed[parts + side], both, pairs))  33.7 us
    ppermute x10, waiting for transfers between devices, shards(): operands.append(lax.ppermute(joined[side], both, pairs))  23.4 us
    ppermute x5, waiting for transfers between devices, shards(): lax.ppermute(packed[turn], 'comp', turns[turn])  18.4 us
    pallas_call x2, Pallas kernels, sweep(): pl.pallas_call(functools.partial(sweep_kernel, parts, [[None] * len(piece...  17.7 us
    pallas_call x5, Pallas kernels, pack(): pl.pallas_call(functools.partial(pack_kernel, parts, rows, low, size, lea...  17.6 us
    pallas_call x5, Pallas kernels, join(): pl.pallas_call(functools.partial(join_kernel, own.shape[0]), out_shape=[s...  17.2 us
  transfers between devices with their start and end apart: 35, of which 13 were waited for; matrix products, arithmetic and copies ran while one was open for 1% of the time, Pallas kernels for 30%

profile of v2, /device:TPU:1, one launch (start us, length us, event | category | flops | bytes accessed | tf_op | source)
XLA Modules:
  0.0 296.6 jit_solution(11027838333602370036)
XLA Ops:
  0.0 0.6 stack.35.scalars
  0.6 3.1 %shard_map.112 = (f32[4,36,8,128]{3,2,1,0:T(8,128)}, f32[4,36,8,128]{3,2,1,0:T(8,128)}, f32[3,36,8,128]{3,2,1,0:T(8,128)}, f32[3,36,8,128]{3,2,1,0:T(8,128)}) custom-call(s32[6]{0:T(128)} %stack.35.scalars, f32[4,36,32,512]{3,2,1,0:T(8,128)} %bitcast.8, s32[32,512]{1,0:T(8,128)} %mask_ref.13), custom_call_target="tpu_custom_call" | custom-call | tf_op jit(solution)/shard_map/pallas_call | solution.py:95
  3.7 2.1 collective-permute-start.27
  5.8 1.0 collective-permute-start.29
  6.8 3.1 %shard_map.109 = (f32[4,36,8,128]{3,2,1,0:T(8,128)}, f32[4,36,8,128]{3,2,1,0:T(8,128)}, f32[3,36,8,128]{3,2,1,0:T(8,128)}, f32[3,36,8,128]{3,2,1,0:T(8,128)}) custom-call(s32[6]{0:T(128)} %stack.35.scalars, f32[4,36,32,512]{3,2,1,0:T(8,128)} %bitcast.9, s32[32,512]{1,0:T(8,128)} %mask_ref.13), custom_call_target="tpu_custom_call" | custom-call | tf_op jit(solution)/shard_map/pallas_call | solution.py:95
  9.9 1.6 collective-permute-start.21
  11.5 1.5 collective-permute-start.23
  13.0 1.2 collective-permute-start.26
  14.3 3.8 %shard_map.106 = (f32[4,36,16,128]{3,2,1,0:T(8,128)}, f32[4,36,16,128]{3,2,1,0:T(8,128)}, f32[3,36,16,128]{3,2,1,0:T(8,128)}, f32[3,36,16,128]{3,2,1,0:T(8,128)}) custom-call(s32[6]{0:T(128)} %stack.35.scalars, f32[4,36,32,512]{3,2,1,0:T(8,128)} %bitcast.10, s32[32,512]{1,0:T(8,128)} %mask_ref.13), custom_call_target="tpu_custom_call" | custom-call | tf_op jit(solution)/shard_map/pallas_call | solution.py:95
  18.2 1.8 collective-permute-start.17
  20.0 5.3 %collective-permute-done.21.refs_2_ = f32[3,36,8,128]{3,2,1,0:T(8,128)S(1)} collective-permute-done((f32[3,36,8,128]{3,2,1,0:T(8,128)}, f32[3,36,8,128]{3,2,1,0:T(8,128)S(1)}, u32[]{:S(2)}, u32[]{:S(2)}) %collective-permute-start.21) | collective-permute-done | bytes 442400 | tf_op jit(solution)/shard_map/ppermute | solution.py:631
  25.4 0.8 copy-done.20
  26.1 1.1 collective-permute-start.20
  27.3 3.8 %shard_map.103 = (f32[4,36,16,128]{3,2,1,0:T(8,128)}, f32[4,36,16,128]{3,2,1,0:T(8,128)}, f32[3,36,16,128]{3,2,1,0:T(8,128)}, f32[3,36,16,128]{3,2,1,0:T(8,128)}) custom-call(s32[6]{0:T(128)} %stack.35.scalars, f32[4,36,32,512]{3,2,1,0:T(8,128)} %bitcast.11, s32[32,512]{1,0:T(8,128)} %mask_ref.13), custom_call_target="tpu_custom_call" | custom-call | tf_op jit(solution)/shard_map/pallas_call | solution.py:95
  31.1 1.4 collective-permute-start.9
  32.7 3.8 %shard_map.100 = (f32[4,36,16,128]{3,2,1,0:T(8,128)}, f32[4,36,16,128]{3,2,1,0:T(8,128)}, f32[3,36,16,128]{3,2,1,0:T(8,128)}, f32[3,36,16,128]{3,2,1,0:T(8,128)}) custom-call(s32[6]{0:T(128)} %stack.35.scalars, f32[4,36,32,512]{3,2,1,0:T(8,128)} %bitcast.12, s32[32,512]{1,0:T(8,128)} %mask_ref.13), custom_call_target="tpu_custom_call" | custom-call | tf_op jit(solution)/shard_map/pallas_call | solution.py:95
  36.5 2.8 collective-permute-done.20.other_ref.refs_1_
  39.2 0.6 collective-permute-start
  39.8 4.6 %collective-permute-done.15.refs_2_ = f32[3,36,16,128]{3,2,1,0:T(8,128)} collective-permute-done((f32[3,36,16,128]{3,2,1,0:T(8,128)}, f32[3,36,16,128]{3,2,1,0:T(8,128)}, u32[]{:S(2)}, u32[]{:S(2)}) %collective-permute-start.15) | collective-permute-done | bytes 884768 | tf_op jit(solution)/shard_map/ppermute | solution.py:631
  44.4 2.2 collective-permute-start.11
  46.9 16.5 %collective-permute-done.9.refs_2_ = f32[3,36,16,128]{3,2,1,0:T(8,128)} collective-permute-done((f32[3,36,16,128]{3,2,1,0:T(8,128)}, f32[3,36,16,128]{3,2,1,0:T(8,128)}, u32[]{:S(2)}, u32[]{:S(2)}) %collective-permute-start.9) | collective-permute-done | bytes 884768 | tf_op jit(solution)/shard_map/ppermute | solution.py:631
  63.4 2.1 collective-permute-start.3
  65.5 3.0 %shard_map.113 = (f32[4,36,8,128]{3,2,1,0:T(8,128)}, f32[4,36,8,128]{3,2,1,0:T(8,128)}) custom-call(s32[6]{0:T(128)} %stack.35.scalars, f32[4,36,8,128]{3,2,1,0:T(8,128)} %get-tuple-element.79.own_ref.refs_0_, f32[4,36,8,128]{3,2,1,0:T(8,128)} %copy-done.11), custom_call_target="tpu_custom_call" | custom-call | tf_op jit(solution)/shard_map/pallas_call | solution.py:139
  68.9 0.6 copy-done.2
  69.5 3.8 %shard_map.104 = (f32[4,36,16,128]{3,2,1,0:T(8,128)}, f32[4,36,16,128]{3,2,1,0:T(8,128)}) custom-call(s32[6]{0:T(128)} %stack.35.scalars, f32[4,36,16,128]{3,2,1,0:T(8,128)} %get-tuple-element.55.own_ref.refs_0_, f32[4,36,16,128]{3,2,1,0:T(8,128)} %copy-done.2), custom_call_target="tpu_custom_call" | custom-call | tf_op jit(solution)/shard_map/pallas_call | solution.py:139
  73.4 1.7 collective-permute-start.14
  75.1 7.3 %collective-permute-done.1.refs_2_ = f32[3,36,16,128]{3,2,1,0:T(8,128)} collective-permute-done((f32[3,36,16,128]{3,2,1,0:T(8,128)}, f32[3,36,16,128]{3,2,1,0:T(8,128)}, u32[]{:S(2)}, u32[]{:S(2)}) %collective-permute-start.1) | collective-permute-done | bytes 884768 | tf_op jit(solution)/shard_map/ppermute | solution.py:631
  82.4 1.2 collective-permute-start.10
  83.5 6.3 %collective-permute-done.other_ref.refs_1_ = f32[4,36,16,128]{3,2,1,0:T(8,128)S(1)} collective-permute-done((f32[4,36,16,128]{3,2,1,0:T(8,128)}, f32[4,36,16,128]{3,2,1,0:T(8,128)S(1)}, u32[]{:S(2)}, u32[]{:S(2)}) %collective-permute-start) | collective-permute-done | bytes 1179680 | tf_op jit(solution)/shard_map/ppermute | solution.py:625
  89.8 5.4 %collective-permute-start.12 = (f32[4,36,16,128]{3,2,1,0:T(8,128)}, f32[4,36,16,128]{3,2,1,0:T(8,128)}, u32[]{:S(2)}, u32[]{:S(2)}) collective-permute-start(f32[4,36,16,128]{3,2,1,0:T(8,128)} %get-tuple-element.60), channel_id=1, source_target_pairs={{0,8},{1,9},{2,4},{3,5},{4,2},{5,3},{6,14},{7,15},{8,0},{9,1},{10,... | collective-permute-start | bytes 3538952 | tf_op jit(solution)/shard_map/ppermute | solution.py:632
  95.2 3.7 %shard_map.101 = (f32[4,36,16,128]{3,2,1,0:T(8,128)}, f32[4,36,16,128]{3,2,1,0:T(8,128)}) custom-call(s32[6]{0:T(128)} %stack.35.scalars, f32[4,36,16,128]{3,2,1,0:T(8,128)} %get-tuple-element.47.own_ref.refs_0_, f32[4,36,16,128]{3,2,1,0:T(8,128)} %copy-done.1), custom_call_target="tpu_custom_call" | custom-call | tf_op jit(solution)/shard_map/pallas_call | solution.py:139
  99.0 3.6 %collective-permute-start.4 = (f32[4,36,16,128]{3,2,1,0:T(8,128)}, f32[4,36,16,128]{3,2,1,0:T(8,128)}, u32[]{:S(2)}, u32[]{:S(2)}) collective-permute-start(f32[4,36,16,128]{3,2,1,0:T(8,128)} %get-tuple-element.52), channel_id=1, source_target_pairs={{0,8},{1,9},{2,4},{3,5},{4,2},{5,3},{6,14},{7,15},{8,0},{9,1},{10,... | collective-permute-start | bytes 3538952 | tf_op jit(solution)/shard_map/ppermute | solution.py:632
  102.6 3.0 %shard_map.110 = (f32[4,36,8,128]{3,2,1,0:T(8,128)}, f32[4,36,8,128]{3,2,1,0:T(8,128)}) custom-call(s32[6]{0:T(128)} %stack.35.scalars, f32[4,36,8,128]{3,2,1,0:T(8,128)} %get-tuple-element.71.own_ref.refs_0_, f32[4,36,8,128]{3,2,1,0:T(8,128)} %copy-done.12), custom_call_target="tpu_custom_call" | custom-call | tf_op jit(solution)/shard_map/pallas_call | solution.py:139
  105.6 9.4 %collective-permute-done.14.other_ref.refs_1_ = f32[4,36,16,128]{3,2,1,0:T(8,128)S(1)} collective-permute-done((f32[4,36,16,128]{3,2,1,0:T(8,128)}, f32[4,36,16,128]{3,2,1,0:T(8,128)S(1)}, u32[]{:S(2)}, u32[]{:S(2)}) %collective-permute-start.14) | collective-permute-done | bytes 1179680 | tf_op jit(solution)/shard_map/ppermute | solution.py:625
  115.0 0.7 collective-permute-start.22
  115.7 4.5 %collective-permute-done.10.refs_3_ = f32[4,36,16,128]{3,2,1,0:T(8,128)S(1)} collective-permute-done((f32[4,36,16,128]{3,2,1,0:T(8,128)}, f32[4,36,16,128]{3,2,1,0:T(8,128)S(1)}, u32[]{:S(2)}, u32[]{:S(2)}) %collective-permute-start.10) | collective-permute-done | bytes 1179680 | tf_op jit(solution)/shard_map/ppermute | solution.py:632
  120.2 2.1 collective-permute-start.24
  122.3 3.7 %shard_map.107 = (f32[4,36,16,128]{3,2,1,0:T(8,128)}, f32[4,36,16,128]{3,2,1,0:T(8,128)}) custom-call(s32[6]{0:T(128)} %stack.35.scalars, f32[4,36,16,128]{3,2,1,0:T(8,128)} %get-tuple-element.63.own_ref.refs_0_, f32[4,36,16,128]{3,2,1,0:T(8,128)} %copy-done), custom_call_target="tpu_custom_call" | custom-call | tf_op jit(solution)/shard_map/pallas_call | solution.py:139
  126.0 0.5 collective-permute-start.16
  126.5 18.9 %collective-permute-done.2.refs_3_ = f32[4,36,16,128]{3,2,1,0:T(8,128)S(1)} collective-permute-done((f32[4,36,16,128]{3,2,1,0:T(8,128)}, f32[4,36,16,128]{3,2,1,0:T(8,128)S(1)}, u32[]{:S(2)}, u32[]{:S(2)}) %collective-permute-start.2) | collective-permute-done | bytes 1179680 | tf_op jit(solution)/shard_map/ppermute | solution.py:632
  145.4 2.1 collective-permute-start.18
  147.6 1.8 sine_multiply_fusion
  149.3 11.6 %shard_map.105 = (f32[4,36,16,128]{3,2,1,0:T(8,128)}, f32[4,36,16,128]{3,2,1,0:T(8,128)}) custom-call(s32[6]{0:T(128)} %stack.35.scalars, f32[32]{0:T(128)} %constant.33.clone.gain_ref, f32[32]{0:T(128)} %constant.34.clone.drop_ref, f32[32,512]{1,0:T(8,128)} %get-tuple-element.90.along_ref, f32[32,512]{1,0:T(8,128)} %get-tuple-element.89.across_ref, ...), custom_call_target="tpu_custom_call" | custom-call | tf_op jit(solution)/shard_map/pallas_call | solution.py:313
  161.2 11.5 %shard_map.102 = (f32[4,36,16,128]{3,2,1,0:T(8,128)}, f32[4,36,16,128]{3,2,1,0:T(8,128)}) custom-call(s32[6]{0:T(128)} %stack.35.scalars, f32[32]{0:T(128)} %constant.33.clone.gain_ref, f32[32]{0:T(128)} %constant.34.clone.drop_ref, f32[32,512]{1,0:T(8,128)} %get-tuple-element.90.along_ref, f32[32,512]{1,0:T(8,128)} %get-tuple-element.89.across_ref, ...), custom_call_target="tpu_custom_call" | custom-call | tf_op jit(solution)/shard_map/pallas_call | solution.py:313
  172.6 1.8 collective-permute-start.13
  174.5 7.5 %shard_map.111 = (f32[4,36,8,128]{3,2,1,0:T(8,128)}, f32[4,36,8,128]{3,2,1,0:T(8,128)}) custom-call(s32[6]{0:T(128)} %stack.35.scalars, f32[32]{0:T(128)} %constant.33.clone.gain_ref, f32[32]{0:T(128)} %constant.34.clone.drop_ref, f32[32,512]{1,0:T(8,128)} %get-tuple-element.90.along_ref, f32[32,512]{1,0:T(8,128)} %get-tuple-element.89.across_ref, ...), custom_call_target="tpu_custom_call" | custom-call | tf_op jit(solution)/shard_map/pallas_call | solution.py:313
  182.0 1.4 collective-permute-start.25
  183.4 7.5 %shard_map.114 = (f32[2,36,8,128]{3,2,1,0:T(8,128)}, f32[2,36,8,128]{3,2,1,0:T(8,128)}, f32[2,36,8,128]{3,2,1,0:T(8,128)}, f32[2,36,8,128]{3,2,1,0:T(8,128)}) custom-call(s32[6]{0:T(128)} %stack.35.scalars, f32[32]{0:T(128)} %constant.33.clone.gain_ref, f32[32]{0:T(128)} %constant.34.clone.drop_ref, f32[32,512]{1,0:T(8,128)} %get-tuple-element.90.along_ref, ...), custom_call_target="tpu_custom_call" | custom-call | tf_op jit(solution)/shard_map/pallas_call | solution.py:313
  191.0 1.0 copy-done.14
  192.0 0.7 collective-permute-start.34
  192.7 11.4 %shard_map.108 = (f32[4,36,16,128]{3,2,1,0:T(8,128)}, f32[4,36,16,128]{3,2,1,0:T(8,128)}) custom-call(s32[6]{0:T(128)} %stack.35.scalars, f32[32]{0:T(128)} %constant.33.clone.gain_ref, f32[32]{0:T(128)} %constant.34.clone.drop_ref, f32[32,512]{1,0:T(8,128)} %get-tuple-element.90.along_ref, f32[32,512]{1,0:T(8,128)} %get-tuple-element.89.across_ref, ...), custom_call_target="tpu_custom_call" | custom-call | tf_op jit(solution)/shard_map/pallas_call | solution.py:313
  204.2 0.8 collective-permute-start.19
  205.0 39.9 %collective-permute-done.34.refs_9_ = f32[2,36,8,128]{3,2,1,0:T(8,128)} collective-permute-done((f32[2,36,8,128]{3,2,1,0:T(8,128)}, f32[2,36,8,128]{3,2,1,0:T(8,128)}, u32[]{:S(2)}, u32[]{:S(2)}) %collective-permute-start.34) | collective-permute-done | bytes 294944 | tf_op jit(solution)/shard_map/ppermute | solution.py:645
  244.9 3.5 %collective-permute-start.32 = (f32[4,36,16,128]{3,2,1,0:T(8,128)S(1)}, f32[4,36,16,128]{3,2,1,0:T(8,128)S(1)}, u32[]{:S(2)}, u32[]{:S(2)}) collective-permute-start(f32[4,36,16,128]{3,2,1,0:T(8,128)S(1)} %copy-done.3), channel_id=1, source_target_pairs={{8,0},{16,8},{24,16},{9,1},{17,9},{25,17},{10,2},{18,10},{26,18},{... | collective-permute-start | bytes 3538952 | tf_op jit(solution)/shard_map/ppermute | solution.py:651
  248.4 3.5 %collective-permute-start.5 = (f32[4,36,16,128]{3,2,1,0:T(8,128)S(1)}, f32[4,36,16,128]{3,2,1,0:T(8,128)S(1)}, u32[]{:S(2)}, u32[]{:S(2)}) collective-permute-start(f32[4,36,16,128]{3,2,1,0:T(8,128)S(1)} %copy-done.4), channel_id=1, source_target_pairs={{0,8},{8,16},{16,24},{1,9},{9,17},{17,25},{2,10},{10,18},{18,26},{... | collective-permute-start | bytes 3538952 | tf_op jit(solution)/shard_map/ppermute | solution.py:651
  251.9 1.9 collective-permute-start.33
  253.8 3.8 %collective-permute-start.7 = (f32[4,36,16,128]{3,2,1,0:T(8,128)}, f32[4,36,16,128]{3,2,1,0:T(8,128)S(1)}, u32[]{:S(2)}, u32[]{:S(2)}) collective-permute-start(f32[4,36,16,128]{3,2,1,0:T(8,128)} %collective-permute-done.6.refs_11_), channel_id=1, source_target_pairs={{0,8},{8,16},{16,24},{1,9},{9,17},{17,25},{2,10},{10,18},{18,26},{... | collective-permute-start | bytes 3538952 | tf_op jit(solution)/shard_map/ppermute | solution.py:651
  257.7 12.4 %collective-permute-done.19.refs_5_ = f32[4,36,16,128]{3,2,1,0:T(8,128)S(1)} collective-permute-done((f32[4,36,16,128]{3,2,1,0:T(8,128)}, f32[4,36,16,128]{3,2,1,0:T(8,128)S(1)}, u32[]{:S(2)}, u32[]{:S(2)}) %collective-permute-start.19) | collective-permute-done | bytes 1179680 | tf_op jit(solution)/shard_map/ppermute | solution.py:645
  270.0 1.2 collective-permute-start.31
  271.3 5.5 %collective-permute-done.33.refs_13_ = f32[4,36,16,128]{3,2,1,0:T(8,128)S(1)} collective-permute-done((f32[4,36,16,128]{3,2,1,0:T(8,128)S(1)}, f32[4,36,16,128]{3,2,1,0:T(8,128)S(1)}, u32[]{:S(2)}, u32[]{:S(2)}) %collective-permute-start.33) | collective-permute-done | bytes 1179680 | tf_op jit(solution)/shard_map/ppermute | solution.py:651
  276.8 0.9 collective-permute-done.7.refs_1_
  277.9 0.9 copy-done.10
  278.8 8.8 %shard_map.115.refs_14_ = f32[4,36,32,512]{3,2,1,0:T(8,128)} custom-call(s32[6]{0:T(128)} %stack.35.scalars, f32[32]{0:T(128)} %constant.35.clone.speed_ref, f32[36]{0:T(128)} %constant.36.clone.cos_ref, f32[36]{0:T(128)} %constant.37.clone.sin_ref, f32[9,32,128]{2,1,0:T(8,128)} %constant.38.clone.geo_ref, s32[32,512]{1,0:T(8,128)} %mask_ref.13, ...), custom_call_target="tpu_custom_call" | custom-call | tf_op jit(solution)/shard_map/pallas_call | solution.py:494
  287.6 8.9 %shard_map.116 = f32[4,36,32,512]{3,2,1,0:T(8,128)} custom-call(s32[6]{0:T(128)} %stack.35.scalars, f32[32]{0:T(128)} %constant.35.clone.speed_ref, f32[36]{0:T(128)} %constant.36.clone.cos_ref, f32[36]{0:T(128)} %constant.37.clone.sin_ref, f32[9,32,128]{2,1,0:T(8,128)} %constant.38.clone.geo_ref, ...), custom_call_target="tpu_custom_call", output_to_operand_aliasing={{}: (20, {})} | custom-call | tf_op jit(solution)/shard_map/pallas_call | solution.py:494
  (73 shorter events, 1.7 us)
Async XLA Ops:
  3.7 14.4 %collective-permute-start.27 = (f32[3,36,8,128]{3,2,1,0:T(8,128)}, f32[3,36,8,128]{3,2,1,0:T(8,128)S(1)}, u32[]{:S(2)}, u32[]{:S(2)}) collective-permute-start(f32[3,36,8,128]{3,2,1,0:T(8,128)} %get-tuple-element.81), channel_id=1, source_target_pairs={{0,2},{1,3},{2,0},{3,1},{4,6},{5,7},{6,4},{7,5},{8,10},{9,11},{10,... | collective-permute-start | bytes 1327112 | tf_op jit(solution)/shard_map/ppermute | solution.py:631
  5.8 7.2 %copy-start.23 = (f32[4,36,8,128]{3,2,1,0:T(8,128)S(1)}, f32[4,36,8,128]{3,2,1,0:T(8,128)}, u32[]{:S(2)}) copy-start(f32[4,36,8,128]{3,2,1,0:T(8,128)} %get-tuple-element.80) | copy-start | bytes 1769476
  5.8 12.4 %collective-permute-start.29 = (f32[3,36,8,128]{3,2,1,0:T(8,128)}, f32[3,36,8,128]{3,2,1,0:T(8,128)S(1)}, u32[]{:S(2)}, u32[]{:S(2)}) collective-permute-start(f32[3,36,8,128]{3,2,1,0:T(8,128)} %get-tuple-element.83), channel_id=1, source_target_pairs={{0,8},{1,9},{2,4},{3,5},{4,2},{5,3},{6,14},{7,15},{8,0},{9,1},{10,... | collective-permute-start | bytes 1327112 | tf_op jit(solution)/shard_map/ppermute | solution.py:631
  9.9 15.5 %collective-permute-start.21 = (f32[3,36,8,128]{3,2,1,0:T(8,128)}, f32[3,36,8,128]{3,2,1,0:T(8,128)S(1)}, u32[]{:S(2)}, u32[]{:S(2)}) collective-permute-start(f32[3,36,8,128]{3,2,1,0:T(8,128)} %get-tuple-element.73), channel_id=1, source_target_pairs={{0,2},{1,3},{2,0},{3,1},{4,6},{5,7},{6,4},{7,5},{8,10},{9,11},{10,... | collective-permute-start | bytes 1327112 | tf_op jit(solution)/shard_map/ppermute | solution.py:631
  11.5 19.6 %collective-permute-start.23 = (f32[3,36,8,128]{3,2,1,0:T(8,128)}, f32[3,36,8,128]{3,2,1,0:T(8,128)S(1)}, u32[]{:S(2)}, u32[]{:S(2)}) collective-permute-start(f32[3,36,8,128]{3,2,1,0:T(8,128)} %get-tuple-element.75), channel_id=1, source_target_pairs={{0,8},{1,9},{2,4},{3,5},{4,2},{5,3},{6,14},{7,15},{8,0},{9,1},{10,... | collective-permute-start | bytes 1327112 | tf_op jit(solution)/shard_map/ppermute | solution.py:631
  13.0 19.4 %collective-permute-start.26 = (f32[4,36,8,128]{3,2,1,0:T(8,128)S(1)}, f32[4,36,8,128]{3,2,1,0:T(8,128)S(1)}, u32[]{:S(2)}, u32[]{:S(2)}) collective-permute-start(f32[4,36,8,128]{3,2,1,0:T(8,128)S(1)} %copy-done.23), channel_id=1, source_target_pairs={{0,1},{1,0},{2,3},{3,2},{4,5},{5,4},{6,7},{7,6},{8,9},{9,8},{10,11... | collective-permute-start | bytes 1769480 | tf_op jit(solution)/shard_map/ppermute | solution.py:625
  18.1 13.0 %copy-start.18 = (f32[3,36,8,128]{3,2,1,0:T(8,128)}, f32[3,36,8,128]{3,2,1,0:T(8,128)S(1)}, u32[]{:S(2)}) copy-start(f32[3,36,8,128]{3,2,1,0:T(8,128)S(1)} %collective-permute-done.27.refs_2_) | copy-start | bytes 1327108
  18.1 26.3 %collective-permute-start.15 = (f32[3,36,16,128]{3,2,1,0:T(8,128)}, f32[3,36,16,128]{3,2,1,0:T(8,128)}, u32[]{:S(2)}, u32[]{:S(2)}) collective-permute-start(f32[3,36,16,128]{3,2,1,0:T(8,128)} %get-tuple-element.65), channel_id=1, source_target_pairs={{0,2},{1,3},{2,0},{3,1},{4,6},{5,7},{6,4},{7,5},{8,10},{9,11},{10,... | collective-permute-start | bytes 2654216 | tf_op jit(solution)/shard_map/ppermute | solution.py:631
  18.2 7.2 %copy-start.19 = (f32[3,36,8,128]{3,2,1,0:T(8,128)}, f32[3,36,8,128]{3,2,1,0:T(8,128)S(1)}, u32[]{:S(2)}) copy-start(f32[3,36,8,128]{3,2,1,0:T(8,128)S(1)} %collective-permute-done.29.refs_4_) | copy-start | bytes 1327108
  18.2 28.4 %collective-permute-start.17 = (f32[3,36,16,128]{3,2,1,0:T(8,128)}, f32[3,36,16,128]{3,2,1,0:T(8,128)}, u32[]{:S(2)}, u32[]{:S(2)}) collective-permute-start(f32[3,36,16,128]{3,2,1,0:T(8,128)} %get-tuple-element.67), channel_id=1, source_target_pairs={{0,8},{1,9},{2,4},{3,5},{4,2},{5,3},{6,14},{7,15},{8,0},{9,1},{10,... | collective-permute-start | bytes 2654216 | tf_op jit(solution)/shard_map/ppermute | solution.py:631
  25.4 0.8 copy-start.20
  26.1 13.1 %collective-permute-start.20 = (f32[4,36,8,128]{3,2,1,0:T(8,128)}, f32[4,36,8,128]{3,2,1,0:T(8,128)S(1)}, u32[]{:S(2)}, u32[]{:S(2)}) collective-permute-start(f32[4,36,8,128]{3,2,1,0:T(8,128)} %get-tuple-element.72), channel_id=1, source_target_pairs={{0,1},{1,0},{2,3},{3,2},{4,5},{5,4},{6,7},{7,6},{8,9},{9,8},{10,11... | collective-permute-start | bytes 1769480 | tf_op jit(solution)/shard_map/ppermute | solution.py:625
  31.1 5.4 %copy-start.21 = (f32[3,36,8,128]{3,2,1,0:T(8,128)}, f32[3,36,8,128]{3,2,1,0:T(8,128)S(1)}, u32[]{:S(2)}) copy-start(f32[3,36,8,128]{3,2,1,0:T(8,128)S(1)} %collective-permute-done.23.refs_4_) | copy-start | bytes 1327108
  31.1 32.3 %collective-permute-start.9 = (f32[3,36,16,128]{3,2,1,0:T(8,128)}, f32[3,36,16,128]{3,2,1,0:T(8,128)}, u32[]{:S(2)}, u32[]{:S(2)}) collective-permute-start(f32[3,36,16,128]{3,2,1,0:T(8,128)} %get-tuple-element.57), channel_id=1, source_target_pairs={{0,2},{1,3},{2,0},{3,1},{4,6},{5,7},{6,4},{7,5},{8,10},{9,11},{10,... | collective-permute-start | bytes 2654216 | tf_op jit(solution)/shard_map/ppermute | solution.py:631
  32.4 4.0 %copy-start.11 = (f32[4,36,8,128]{3,2,1,0:T(8,128)}, f32[4,36,8,128]{3,2,1,0:T(8,128)S(1)}, u32[]{:S(2)}) copy-start(f32[4,36,8,128]{3,2,1,0:T(8,128)S(1)} %collective-permute-done.26.other_ref.refs_1_) | copy-start | bytes 1769476
  32.4 36.1 %collective-permute-start.8 = (f32[4,36,16,128]{3,2,1,0:T(8,128)}, f32[4,36,16,128]{3,2,1,0:T(8,128)S(1)}, u32[]{:S(2)}, u32[]{:S(2)}) collective-permute-start(f32[4,36,16,128]{3,2,1,0:T(8,128)} %get-tuple-element.56), channel_id=1, source_target_pairs={{0,1},{1,0},{2,3},{3,2},{4,5},{5,4},{6,7},{7,6},{8,9},{9,8},{10,11... | collective-permute-start | bytes 3538952 | tf_op jit(solution)/shard_map/ppermute | solution.py:625
  39.2 34.1 %copy-start.12 = (f32[4,36,8,128]{3,2,1,0:T(8,128)}, f32[4,36,8,128]{3,2,1,0:T(8,128)S(1)}, u32[]{:S(2)}) copy-start(f32[4,36,8,128]{3,2,1,0:T(8,128)S(1)} %collective-permute-done.20.other_ref.refs_1_) | copy-start | bytes 1769476
  39.2 50.6 %collective-permute-start = (f32[4,36,16,128]{3,2,1,0:T(8,128)}, f32[4,36,16,128]{3,2,1,0:T(8,128)S(1)}, u32[]{:S(2)}, u32[]{:S(2)}) collective-permute-start(f32[4,36,16,128]{3,2,1,0:T(8,128)} %get-tuple-element.48), channel_id=1, source_target_pairs={{0,1},{1,0},{2,3},{3,2},{4,5},{5,4},{6,7},{7,6},{8,9},{9,8},{10,11... | collective-permute-start | bytes 3538952 | tf_op jit(solution)/shard_map/ppermute | solution.py:625
  44.4 28.9 %collective-permute-start.11 = (f32[3,36,16,128]{3,2,1,0:T(8,128)}, f32[3,36,16,128]{3,2,1,0:T(8,128)}, u32[]{:S(2)}, u32[]{:S(2)}) collective-permute-start(f32[3,36,16,128]{3,2,1,0:T(8,128)} %get-tuple-element.59), channel_id=1, source_target_pairs={{0,8},{1,9},{2,4},{3,5},{4,2},{5,3},{6,14},{7,15},{8,0},{9,1},{10,... | collective-permute-start | bytes 2654216 | tf_op jit(solution)/shard_map/ppermute | solution.py:631
  46.6 35.7 %collective-permute-start.1 = (f32[3,36,16,128]{3,2,1,0:T(8,128)}, f32[3,36,16,128]{3,2,1,0:T(8,128)}, u32[]{:S(2)}, u32[]{:S(2)}) collective-permute-start(f32[3,36,16,128]{3,2,1,0:T(8,128)} %get-tuple-element.49), channel_id=1, source_target_pairs={{0,2},{1,3},{2,0},{3,1},{4,6},{5,7},{6,4},{7,5},{8,10},{9,11},{10,... | collective-permute-start | bytes 2654216 | tf_op jit(solution)/shard_map/ppermute | solution.py:631
  63.4 35.5 %collective-permute-start.3 = (f32[3,36,16,128]{3,2,1,0:T(8,128)}, f32[3,36,16,128]{3,2,1,0:T(8,128)}, u32[]{:S(2)}, u32[]{:S(2)}) collective-permute-start(f32[3,36,16,128]{3,2,1,0:T(8,128)} %get-tuple-element.51), channel_id=1, source_target_pairs={{0,8},{1,9},{2,4},{3,5},{4,2},{5,3},{6,14},{7,15},{8,0},{9,1},{10,... | collective-permute-start | bytes 2654216 | tf_op jit(solution)/shard_map/ppermute | solution.py:631
  68.5 1.1 copy-start.2
  68.5 30.5 %collective-permute-start.28 = (f32[4,36,8,128]{3,2,1,0:T(8,128)}, f32[4,36,8,128]{3,2,1,0:T(8,128)}, u32[]{:S(2)}, u32[]{:S(2)}) collective-permute-start(f32[4,36,8,128]{3,2,1,0:T(8,128)} %get-tuple-element.82), channel_id=1, source_target_pairs={{0,2},{1,3},{2,0},{3,1},{4,6},{5,7},{6,4},{7,5},{8,10},{9,11},{10,... | collective-permute-start | bytes 1769480 | tf_op jit(solution)/shard_map/ppermute | solution.py:632
  73.4 41.6 %collective-permute-start.14 = (f32[4,36,16,128]{3,2,1,0:T(8,128)}, f32[4,36,16,128]{3,2,1,0:T(8,128)S(1)}, u32[]{:S(2)}, u32[]{:S(2)}) collective-permute-start(f32[4,36,16,128]{3,2,1,0:T(8,128)} %get-tuple-element.64), channel_id=1, source_target_pairs={{0,1},{1,0},{2,3},{3,2},{4,5},{5,4},{6,7},{7,6},{8,9},{9,8},{10,11... | collective-permute-start | bytes 3538952 | tf_op jit(solution)/shard_map/ppermute | solution.py:625
  82.4 37.8 %collective-permute-start.10 = (f32[4,36,16,128]{3,2,1,0:T(8,128)}, f32[4,36,16,128]{3,2,1,0:T(8,128)S(1)}, u32[]{:S(2)}, u32[]{:S(2)}) collective-permute-start(f32[4,36,16,128]{3,2,1,0:T(8,128)} %get-tuple-element.58), channel_id=1, source_target_pairs={{0,2},{1,3},{2,0},{3,1},{4,6},{5,7},{6,4},{7,5},{8,10},{9,11},{10,... | collective-permute-start | bytes 3538952 | tf_op jit(solution)/shard_map/ppermute | solution.py:632
  89.8 5.4 %copy-start.1 = (f32[4,36,16,128]{3,2,1,0:T(8,128)}, f32[4,36,16,128]{3,2,1,0:T(8,128)S(1)}, u32[]{:S(2)}) copy-start(f32[4,36,16,128]{3,2,1,0:T(8,128)S(1)} %collective-permute-done.other_ref.refs_1_) | copy-start | bytes 3538948
  89.8 36.2 %collective-permute-start.12 = (f32[4,36,16,128]{3,2,1,0:T(8,128)}, f32[4,36,16,128]{3,2,1,0:T(8,128)}, u32[]{:S(2)}, u32[]{:S(2)}) collective-permute-start(f32[4,36,16,128]{3,2,1,0:T(8,128)} %get-tuple-element.60), channel_id=1, source_target_pairs={{0,8},{1,9},{2,4},{3,5},{4,2},{5,3},{6,14},{7,15},{8,0},{9,1},{10,... | collective-permute-start | bytes 3538952 | tf_op jit(solution)/shard_map/ppermute | solution.py:632
  98.9 46.5 %collective-permute-start.2 = (f32[4,36,16,128]{3,2,1,0:T(8,128)}, f32[4,36,16,128]{3,2,1,0:T(8,128)S(1)}, u32[]{:S(2)}, u32[]{:S(2)}) collective-permute-start(f32[4,36,16,128]{3,2,1,0:T(8,128)} %get-tuple-element.50), channel_id=1, source_target_pairs={{0,2},{1,3},{2,0},{3,1},{4,6},{5,7},{6,4},{7,5},{8,10},{9,11},{10,... | collective-permute-start | bytes 3538952 | tf_op jit(solution)/shard_map/ppermute | solution.py:632
  99.0 61.9 %collective-permute-start.4 = (f32[4,36,16,128]{3,2,1,0:T(8,128)}, f32[4,36,16,128]{3,2,1,0:T(8,128)}, u32[]{:S(2)}, u32[]{:S(2)}) collective-permute-start(f32[4,36,16,128]{3,2,1,0:T(8,128)} %get-tuple-element.52), channel_id=1, source_target_pairs={{0,8},{1,9},{2,4},{3,5},{4,2},{5,3},{6,14},{7,15},{8,0},{9,1},{10,... | collective-permute-start | bytes 3538952 | tf_op jit(solution)/shard_map/ppermute | solution.py:632
  115.0 7.3 %copy-start = (f32[4,36,16,128]{3,2,1,0:T(8,128)}, f32[4,36,16,128]{3,2,1,0:T(8,128)S(1)}, u32[]{:S(2)}) copy-start(f32[4,36,16,128]{3,2,1,0:T(8,128)S(1)} %collective-permute-done.14.other_ref.refs_1_) | copy-start | bytes 3538948
  115.0 57.6 %collective-permute-start.22 = (f32[4,36,8,128]{3,2,1,0:T(8,128)}, f32[4,36,8,128]{3,2,1,0:T(8,128)}, u32[]{:S(2)}, u32[]{:S(2)}) collective-permute-start(f32[4,36,8,128]{3,2,1,0:T(8,128)} %get-tuple-element.74), channel_id=1, source_target_pairs={{0,2},{1,3},{2,0},{3,1},{4,6},{5,7},{6,4},{7,5},{8,10},{9,11},{10,... | collective-permute-start | bytes 1769480 | tf_op jit(solution)/shard_map/ppermute | solution.py:632
  120.2 5.8 %copy-start.15 = (f32[4,36,16,128]{3,2,1,0:T(8,128)}, f32[4,36,16,128]{3,2,1,0:T(8,128)S(1)}, u32[]{:S(2)}) copy-start(f32[4,36,16,128]{3,2,1,0:T(8,128)S(1)} %collective-permute-done.10.refs_3_) | copy-start | bytes 3538948
  120.2 54.2 %collective-permute-start.24 = (f32[4,36,8,128]{3,2,1,0:T(8,128)}, f32[4,36,8,128]{3,2,1,0:T(8,128)}, u32[]{:S(2)}, u32[]{:S(2)}) collective-permute-start(f32[4,36,8,128]{3,2,1,0:T(8,128)} %get-tuple-element.76), channel_id=1, source_target_pairs={{0,8},{1,9},{2,4},{3,5},{4,2},{5,3},{6,14},{7,15},{8,0},{9,1},{10,... | collective-permute-start | bytes 1769480 | tf_op jit(solution)/shard_map/ppermute | solution.py:632
  126.0 65.0 %collective-permute-start.16 = (f32[4,36,16,128]{3,2,1,0:T(8,128)}, f32[4,36,16,128]{3,2,1,0:T(8,128)S(1)}, u32[]{:S(2)}, u32[]{:S(2)}) collective-permute-start(f32[4,36,16,128]{3,2,1,0:T(8,128)} %get-tuple-element.66), channel_id=1, source_target_pairs={{0,2},{1,3},{2,0},{3,1},{4,6},{5,7},{6,4},{7,5},{8,10},{9,11},{10,... | collective-permute-start | bytes 3538952 | tf_op jit(solution)/shard_map/ppermute | solution.py:632
  145.4 15.5 %copy-start.16 = (f32[4,36,16,128]{3,2,1,0:T(8,128)}, f32[4,36,16,128]{3,2,1,0:T(8,128)S(1)}, u32[]{:S(2)}) copy-start(f32[4,36,16,128]{3,2,1,0:T(8,128)S(1)} %collective-permute-done.2.refs_3_) | copy-start | bytes 3538948
  145.4 47.3 %collective-permute-start.18 = (f32[4,36,16,128]{3,2,1,0:T(8,128)}, f32[4,36,16,128]{3,2,1,0:T(8,128)}, u32[]{:S(2)}, u32[]{:S(2)}) collective-permute-start(f32[4,36,16,128]{3,2,1,0:T(8,128)} %get-tuple-element.68), channel_id=1, source_target_pairs={{0,8},{1,9},{2,4},{3,5},{4,2},{5,3},{6,14},{7,15},{8,0},{9,1},{10,... | collective-permute-start | bytes 3538952 | tf_op jit(solution)/shard_map/ppermute | solution.py:632
  149.3 11.6 %copy-start.22 = (f32[4,36,8,128]{3,2,1,0:T(8,128)S(1)}, f32[4,36,8,128]{3,2,1,0:T(8,128)}, u32[]{:S(2)}) copy-start(f32[4,36,8,128]{3,2,1,0:T(8,128)} %get-tuple-element.84) | copy-start | bytes 1769476
  160.9 21.0 %collective-permute-start.30 = (f32[4,36,8,128]{3,2,1,0:T(8,128)S(1)}, f32[4,36,8,128]{3,2,1,0:T(8,128)S(1)}, u32[]{:S(2)}, u32[]{:S(2)}) collective-permute-start(f32[4,36,8,128]{3,2,1,0:T(8,128)S(1)} %copy-done.22), channel_id=1, source_target_pairs={{0,8},{1,9},{2,4},{3,5},{4,2},{5,3},{6,14},{7,15},{8,0},{9,1},{10,... | collective-permute-start | bytes 1769480 | tf_op jit(solution)/shard_map/ppermute | solution.py:632
  172.6 79.2 %collective-permute-start.13 = (f32[4,36,16,128]{3,2,1,0:T(8,128)}, f32[4,36,16,128]{3,2,1,0:T(8,128)S(1)}, u32[]{:S(2)}, u32[]{:S(2)}) collective-permute-start(f32[4,36,16,128]{3,2,1,0:T(8,128)} %get-tuple-element.62), channel_id=1, source_target_pairs={{1,0},{0,1},{3,2},{2,3},{5,4},{4,5},{7,6},{6,7},{9,8},{8,9},{11,10... | collective-permute-start | bytes 3538952 | tf_op jit(solution)/shard_map/ppermute | solution.py:645
  174.4 79.4 %collective-permute-start.6 = (f32[4,36,16,128]{3,2,1,0:T(8,128)}, f32[4,36,16,128]{3,2,1,0:T(8,128)}, u32[]{:S(2)}, u32[]{:S(2)}) collective-permute-start(f32[4,36,16,128]{3,2,1,0:T(8,128)} %get-tuple-element.54), channel_id=1, source_target_pairs={{1,0},{0,1},{3,2},{2,3},{5,4},{4,5},{7,6},{6,7},{9,8},{8,9},{11,10... | collective-permute-start | bytes 3538952 | tf_op jit(solution)/shard_map/ppermute | solution.py:645
  182.0 1.5 copy-start.17
  182.0 66.4 %collective-permute-start.25 = (f32[4,36,8,128]{3,2,1,0:T(8,128)}, f32[4,36,8,128]{3,2,1,0:T(8,128)S(1)}, u32[]{:S(2)}, u32[]{:S(2)}) collective-permute-start(f32[4,36,8,128]{3,2,1,0:T(8,128)} %get-tuple-element.78), channel_id=1, source_target_pairs={{1,0},{0,1},{3,2},{2,3},{5,4},{4,5},{7,6},{6,7},{9,8},{8,9},{11,10... | collective-permute-start | bytes 1769480 | tf_op jit(solution)/shard_map/ppermute | solution.py:645
  191.0 1.0 copy-start.14
  192.0 52.9 %copy-start.3 = (f32[4,36,16,128]{3,2,1,0:T(8,128)S(1)}, f32[4,36,16,128]{3,2,1,0:T(8,128)}, u32[]{:S(2)}) copy-start(f32[4,36,16,128]{3,2,1,0:T(8,128)} %get-tuple-element.61.refs_2_) | copy-start | bytes 3538948
  192.0 56.4 %copy-start.4 = (f32[4,36,16,128]{3,2,1,0:T(8,128)S(1)}, f32[4,36,16,128]{3,2,1,0:T(8,128)}, u32[]{:S(2)}) copy-start(f32[4,36,16,128]{3,2,1,0:T(8,128)} %get-tuple-element.53.refs_10_) | copy-start | bytes 3538948
  192.0 52.9 %collective-permute-start.34 = (f32[2,36,8,128]{3,2,1,0:T(8,128)}, f32[2,36,8,128]{3,2,1,0:T(8,128)}, u32[]{:S(2)}, u32[]{:S(2)}) collective-permute-start(f32[2,36,8,128]{3,2,1,0:T(8,128)} %get-tuple-element.88), channel_id=1, source_target_pairs={{1,0},{0,1},{3,2},{2,3},{5,4},{4,5},{7,6},{6,7},{9,8},{8,9},{11,10... | collective-permute-start | bytes 884744 | tf_op jit(solution)/shard_map/ppermute | solution.py:645
  204.2 65.9 %collective-permute-start.19 = (f32[4,36,16,128]{3,2,1,0:T(8,128)}, f32[4,36,16,128]{3,2,1,0:T(8,128)S(1)}, u32[]{:S(2)}, u32[]{:S(2)}) collective-permute-start(f32[4,36,16,128]{3,2,1,0:T(8,128)} %get-tuple-element.70), channel_id=1, source_target_pairs={{1,0},{0,1},{3,2},{2,3},{5,4},{4,5},{7,6},{6,7},{9,8},{8,9},{11,10... | collective-permute-start | bytes 3538952 | tf_op jit(solution)/shard_map/ppermute | solution.py:645
  244.9 26.4 %collective-permute-start.32 = (f32[4,36,16,128]{3,2,1,0:T(8,128)S(1)}, f32[4,36,16,128]{3,2,1,0:T(8,128)S(1)}, u32[]{:S(2)}, u32[]{:S(2)}) collective-permute-start(f32[4,36,16,128]{3,2,1,0:T(8,128)S(1)} %copy-done.3), channel_id=1, source_target_pairs={{8,0},{16,8},{24,16},{9,1},{17,9},{25,17},{10,2},{18,10},{26,18},{... | collective-permute-start | bytes 3538952 | tf_op jit(solution)/shard_map/ppermute | solution.py:651
  248.4 30.4 %copy-start.13 = (f32[4,36,8,128]{3,2,1,0:T(8,128)}, f32[4,36,8,128]{3,2,1,0:T(8,128)S(1)}, u32[]{:S(2)}) copy-start(f32[4,36,8,128]{3,2,1,0:T(8,128)S(1)} %collective-permute-done.25.refs_7_) | copy-start | bytes 1769476
  248.4 22.9 %collective-permute-start.5 = (f32[4,36,16,128]{3,2,1,0:T(8,128)S(1)}, f32[4,36,16,128]{3,2,1,0:T(8,128)S(1)}, u32[]{:S(2)}, u32[]{:S(2)}) collective-permute-start(f32[4,36,16,128]{3,2,1,0:T(8,128)S(1)} %copy-done.4), channel_id=1, source_target_pairs={{0,8},{8,16},{16,24},{1,9},{9,17},{17,25},{2,10},{10,18},{18,26},{... | collective-permute-start | bytes 3538952 | tf_op jit(solution)/shard_map/ppermute | solution.py:651
  251.9 26.9 %copy-start.5 = (f32[4,36,16,128]{3,2,1,0:T(8,128)}, f32[4,36,16,128]{3,2,1,0:T(8,128)S(1)}, u32[]{:S(2)}) copy-start(f32[4,36,16,128]{3,2,1,0:T(8,128)S(1)} %collective-permute-done.13.refs_3_) | copy-start | bytes 3538948
  251.9 24.9 %collective-permute-start.33 = (f32[4,36,16,128]{3,2,1,0:T(8,128)S(1)}, f32[4,36,16,128]{3,2,1,0:T(8,128)S(1)}, u32[]{:S(2)}, u32[]{:S(2)}) collective-permute-start(f32[4,36,16,128]{3,2,1,0:T(8,128)S(1)} %collective-permute-done.13.refs_3_), channel_id=1, source_target_pairs={{8,0},{16,8},{24,16},{9,1},{17,9},{25,17},{10,2},{18,10},{26,18},{... | collective-permute-start | bytes 3538952 | tf_op jit(solution)/shard_map/ppermute | solution.py:651
  253.8 23.9 %collective-permute-start.7 = (f32[4,36,16,128]{3,2,1,0:T(8,128)}, f32[4,36,16,128]{3,2,1,0:T(8,128)S(1)}, u32[]{:S(2)}, u32[]{:S(2)}) collective-permute-start(f32[4,36,16,128]{3,2,1,0:T(8,128)} %collective-permute-done.6.refs_11_), channel_id=1, source_target_pairs={{0,8},{8,16},{16,24},{1,9},{9,17},{17,25},{2,10},{10,18},{18,26},{... | collective-permute-start | bytes 3538952 | tf_op jit(solution)/shard_map/ppermute | solution.py:651
  270.0 6.8 %copy-start.6 = (f32[4,36,16,128]{3,2,1,0:T(8,128)}, f32[4,36,16,128]{3,2,1,0:T(8,128)S(1)}, u32[]{:S(2)}) copy-start(f32[4,36,16,128]{3,2,1,0:T(8,128)S(1)} %collective-permute-done.19.refs_5_) | copy-start | bytes 3538948
  270.0 17.6 %collective-permute-start.31 = (f32[2,36,8,128]{3,2,1,0:T(8,128)}, f32[2,36,8,128]{3,2,1,0:T(8,128)}, u32[]{:S(2)}, u32[]{:S(2)}) collective-permute-start(f32[2,36,8,128]{3,2,1,0:T(8,128)} %get-tuple-element.86), channel_id=1, source_target_pairs={{1,0},{0,1},{3,2},{2,3},{5,4},{4,5},{7,6},{6,7},{9,8},{8,9},{11,10... | collective-permute-start | bytes 884744 | tf_op jit(solution)/shard_map/ppermute | solution.py:645
  271.3 6.5 %copy-start.7 = (f32[4,36,16,128]{3,2,1,0:T(8,128)}, f32[4,36,16,128]{3,2,1,0:T(8,128)S(1)}, u32[]{:S(2)}) copy-start(f32[4,36,16,128]{3,2,1,0:T(8,128)S(1)} %collective-permute-done.32.refs_12_) | copy-start | bytes 3538948
  271.3 6.5 %copy-start.8 = (f32[4,36,16,128]{3,2,1,0:T(8,128)}, f32[4,36,16,128]{3,2,1,0:T(8,128)S(1)}, u32[]{:S(2)}) copy-start(f32[4,36,16,128]{3,2,1,0:T(8,128)S(1)} %collective-permute-done.5.refs_0_) | copy-start | bytes 3538948
  276.8 1.1 copy-start.9
  277.7 1.0 copy-start.10
